TPU v7x, 128 devices: a whole 4x4x4 slice. The times are simulated.
128 devices in a mesh: gx: 32 (over z, y, core), gz: 4 (over x).
Axes of the slice: x: 4, y: 4, z: 4, core: 2. Of those that a mesh axis runs over, the one named last changes fastest.
Arguments:
- parents: bfloat16 [35, 8, 524288], P(None, None, ('gx', 'gz')), may hold values from -6 to 6
- refine: int32 [524288], P(('gx', 'gz')), may hold values 0 or 1
- edge: int32 [524288], P(('gx', 'gz')), may hold values from 0 to 5
- move: int32 [524288], P(('gx', 'gz')), may hold values from 0 to 6, as said below
- face_owner: int32 [4, 128, 1024], P(None, ('gx', 'gz')), may hold values from 0 to 4095
- face_local: int32 [4, 128, 1024], P(None, ('gx', 'gz')), may hold values from 0 to 3
- face_pair: int32 [4, 128, 1024], P(None, ('gx', 'gz')), may hold values from 0 to 1023, each once within a row
- face_orient: int32 [4, 128, 1024], P(None, ('gx', 'gz')), may hold values from 0 to 5
- prolong: bfloat16 [6, 2, 35, 35], replicated, may hold values from -1 to 1
- restrict: bfloat16 [4, 15, 35], replicated, may hold values from -1 to 1
- lift: float32 [4, 35, 15], replicated, may hold values from -1.5 to 1.5
Outputs:
- migrated: bfloat16 [2, 35, 8, 720896], P(None, None, None, ('gx', 'gz'))
Inputs may be any that keep to these rules, and one draw needn't show every extreme that they name: Each row of face_pair is a permutation of the neighbour's 1024 faces on the matching side. Among the 4096 parents of one device at most 256 have the same move k < 6, and on every device some k reaches exactly 256.
All inputs are finite; a program needn't handle non-finite values. No bound on the sum of `refine` on one device may be relied on, other than what follows from the above.
Results may differ from a plain program's by a relative error of at most 0.005.
Values may be sent and summed in bfloat16 or wider, within the bound.
No kernel may reach another device: no remote copies, remote signals or barrier semaphores. Data moves between devices by JAX's collectives and lax.ppermute only.
A program may use at most 128 MiB of HBM per device.

v0:
```python
import functools

import jax
import jax.numpy as jnp
from jax import lax
from jax.experimental import pallas as pl
from jax.experimental.pallas import tpu as pltpu
from jax.sharding import PartitionSpec as P

MODES = 35
FMODES = 15
FIELDS = 8
ROWS = MODES * FIELDS
NODE_ROWS = FMODES * FIELDS
PAD = 40
LANES = 128
BUCKET = 512
WINDOW = 256
TILE = 512
LIMIT = 30 << 20
OFFSETS = (1, 2, 3, -1, -2, -3)
F32 = jnp.float32
BF16 = jnp.bfloat16
NT = (((1,), (1,)), ((), ()))


def passed_along(block, axis, distance):
    count = lax.axis_size(axis)
    return lax.ppermute(block, axis, [((i - distance) % count, i) for i in range(count)])


def face_table():
    nodes = [(a, b, 4 - a - b) for a in range(5) for b in range(5 - a)]
    index = {node: place for place, node in enumerate(nodes)}
    orders = [(0, 1, 2), (1, 2, 0), (2, 0, 1), (1, 0, 2), (0, 2, 1), (2, 1, 0)]
    return [[index[n[p[0]], n[p[1]], n[p[2]]] for n in nodes] for p in orders]


def iota(shape, dim):
    return lax.broadcasted_iota(jnp.int32, shape, dim)


def ones_where(mask):
    return jnp.where(mask, 1.0, 0.0).astype(BF16)


def match(rows, row):
    shape = (rows, row.shape[1])
    lines = lax.broadcasted_iota(jnp.int16, shape, 0)
    same = lines == jnp.broadcast_to(row.astype(jnp.int16), shape)
    return jnp.where(same, jnp.array(1, BF16), jnp.array(0, BF16))


def dot(a, b):
    return jnp.dot(a, b, preferred_element_type=F32)


def spread(small, rows, columns):
    height, width = small.shape
    left = ones_where(iota((rows, height), 0) // FIELDS == iota((rows, height), 1))
    right = ones_where(iota((width, columns), 0) == iota((width, columns), 1) // FIELDS)
    full = dot(dot(left, small).astype(BF16), right)
    same = iota((rows, columns), 0) % FIELDS == iota((rows, columns), 1) % FIELDS
    return jnp.where(same, full, 0.0)


VMEM_SPEC = pl.BlockSpec(memory_space=pltpu.VMEM)
SMEM_SPEC = pl.BlockSpec(memory_space=pltpu.SMEM)
HBM_SPEC = pl.BlockSpec(memory_space=pltpu.HBM)


def fetches(sources, targets, sems):
    copies = [pltpu.make_async_copy(a, b, sems.at[i]) for i, (a, b) in enumerate(zip(sources, targets))]
    for copy in copies:
        copy.start()
    return copies


def room(*arrays):
    buffers = [pltpu.VMEM(a.shape, a.dtype) for a in arrays]
    return buffers + [pltpu.SemaphoreType.DMA((len(arrays),))]


def trace_kernel(tile, *refs):
    sources, own_refs, every_ref, held, sems = refs[:4], refs[4:8], refs[8], refs[9:13], refs[13]
    restrict_ref, owner_ref, local_ref, x_ref = held
    copies = fetches(sources, held, sems)
    count = x_ref.shape[1]
    faces = owner_ref.shape[2]
    copies[0].wait()
    spreads = [spread(restrict_ref[:, l, :], NODE_ROWS, ROWS) for l in range(4)]
    every_ref[...] = jnp.concatenate(spreads, axis=0).astype(BF16)
    for copy in copies[1:]:
        copy.wait()
    for s in range(4):

        def step(j, carry, s=s):
            lanes = pl.ds(pl.multiple_of(j * tile, tile), tile)
            owner = owner_ref[s, :, lanes]
            local = local_ref[s, :, lanes]
            onehot = match(count, owner)
            picked = dot(x_ref[...], onehot).astype(BF16)
            traces = dot(every_ref[...], picked)
            chosen = traces[:NODE_ROWS]
            for l in range(1, 4):
                chosen = jnp.where(local == l, traces[l * NODE_ROWS : (l + 1) * NODE_ROWS], chosen)
            own_refs[s][:, lanes] = chosen.astype(BF16)
            return carry

        lax.fori_loop(0, faces // tile, step, 0)


def trace_call(x, owner, local, restrict):
    faces = owner.shape[2]
    return pl.pallas_call(
        functools.partial(trace_kernel, 1024),
        in_specs=[HBM_SPEC] * 4,
        out_specs=[VMEM_SPEC] * 4,
        out_shape=[jax.ShapeDtypeStruct((NODE_ROWS, faces), BF16)] * 4,
        scratch_shapes=[pltpu.VMEM((4 * NODE_ROWS, ROWS), BF16)] + room(restrict, owner, local, x),
        compiler_params=pltpu.CompilerParams(vmem_limit_bytes=LIMIT),
        cost_estimate=pl.CostEstimate(flops=10**10, bytes_accessed=10**7, transcendentals=0),
        name="trace",
    )(*[pltpu.with_memory_space_constraint(a, pltpu.HBM) for a in (restrict, owner, local, x)])


def rank_moves(move_ref, refine_ref, edge_ref, place_ref, code_ref, state_ref):
    count = move_ref.shape[1]
    block = 256
    cap = count // 16
    before = ones_where(iota((block, block), 0) < iota((block, block), 1))
    seen = jnp.zeros((8, 1), F32)
    which = iota((8, block), 0)
    for b in range(count // block):
        at = slice(b * block, (b + 1) * block)
        move = move_ref[:, at]
        hit = jnp.where(which == move, 1.0, 0.0)
        earlier = dot(hit.astype(BF16), before) + seen
        rank = jnp.sum(hit * earlier, axis=0, keepdims=True).astype(jnp.int32)
        place_ref[:, at] = jnp.where(move < 6, move * cap + rank, 6 * cap)
        seen = seen + jnp.sum(hit, axis=1, keepdims=True)
        code = jnp.where(refine_ref[:, at] == 1, edge_ref[:, at] + 1, 0)
        code_ref[:, at] = code
        state_ref[:, at] = jnp.where(move == 6, code, -1)


def plan_kernel(*refs):
    own_refs, sources, held, sems = refs[:4], refs[4:12], refs[19:27], refs[27]
    own_ref, meta_ref, table_ref, raised_ref, place_ref, code_ref, state_ref = refs[12:19]
    owner_ref, local_ref, pair_ref, orient_ref, lift_ref, move_ref, refine_ref, edge_ref = held
    for copy in fetches(sources, held, sems):
        copy.wait()
    rank_moves(move_ref, refine_ref, edge_ref, place_ref, code_ref, state_ref)
    raised = [spread(lift_ref[:, l, :].astype(BF16), NODE_ROWS, ROWS) for l in range(4)]
    raised_ref[...] = jnp.concatenate(raised, axis=0).T.astype(BF16)
    faces = owner_ref.shape[2]
    block = 256
    before = ones_where(iota((block, block), 0) < iota((block, block), 1))
    eight = iota((8, faces), 0)
    buckets = [owner_ref[s] // BUCKET for s in range(4)]
    hits = jnp.concatenate([jnp.where(eight == b, 1.0, 0.0) for b in buckets], axis=0)
    smaller = jnp.concatenate([jnp.where(b < eight, 1.0, 0.0) for b in buckets], axis=0)
    start = jnp.sum(smaller, axis=1, keepdims=True)
    end = start + jnp.sum(hits, axis=1, keepdims=True)
    first = start.astype(jnp.int32)
    last = end.astype(jnp.int32)
    begin = jnp.minimum(first // LANES * LANES, faces - LANES)
    trips = (last - begin + WINDOW - 1) // WINDOW
    longest = jnp.maximum(
        jnp.maximum(trips[0:8], trips[8:16]), jnp.maximum(trips[16:24], trips[24:32])
    )
    longest = jnp.concatenate([longest] * 4, axis=0)
    lane = iota((32, LANES), 1)
    table_ref[...] = jnp.where(lane == 0, begin, jnp.where(lane == 1, trips, longest))
    seen = start
    places = []
    for b in range(faces // block):
        part = hits[:, b * block : (b + 1) * block]
        places.append(part * (dot(part.astype(BF16), before) + seen))
        seen = seen + jnp.sum(part, axis=1, keepdims=True)
    places = jnp.concatenate(places, axis=1)
    meta_ref[...] = jnp.full(meta_ref.shape, -1, jnp.int32)
    for s in range(4):
        spot = jnp.sum(places[8 * s : 8 * s + 8], axis=0, keepdims=True).astype(jnp.int32)
        order = match(faces, spot)
        owner, pair = owner_ref[s], pair_ref[s]
        values = (owner // 256, owner % 256, local_ref[s], pair // 256, pair % 256, orient_ref[s])
        small = jnp.zeros((8, faces), jnp.int32)
        for row, value in enumerate(values):
            small = jnp.where(eight == row, value, small)
        both = jnp.concatenate([own_refs[s][...].astype(F32), small.astype(F32)], axis=0)
        moved = lax.dot_general(both.astype(BF16), order, NT, preferred_element_type=F32)
        own_ref[s] = moved[:NODE_ROWS].astype(BF16)
        got = moved[NODE_ROWS:].astype(jnp.int32)
        rows = (got[0:1] * 256 + got[1:2], got[2:3], got[3:4] * 256 + got[4:5], got[5:6])
        meta = jnp.zeros((8, faces), jnp.int32)
        for row, value in enumerate(rows):
            meta = jnp.where(eight == row, value, meta)
        meta_ref[s, :, :faces] = meta


def plan_call(owns, *rest):
    faces = rest[0].shape[2]
    flat = jax.ShapeDtypeStruct(rest[-1].shape, jnp.int32)
    return pl.pallas_call(
        plan_kernel,
        in_specs=[VMEM_SPEC] * 4 + [HBM_SPEC] * 8,
        out_specs=[VMEM_SPEC] * 7,
        out_shape=[
            jax.ShapeDtypeStruct((4, NODE_ROWS, faces), BF16),
            jax.ShapeDtypeStruct((4, 8, faces + LANES), jnp.int32),
            jax.ShapeDtypeStruct((32, LANES), jnp.int32),
            jax.ShapeDtypeStruct((ROWS, 4 * NODE_ROWS), BF16),
            flat,
            flat,
            flat,
        ],
        scratch_shapes=room(*rest),
        compiler_params=pltpu.CompilerParams(vmem_limit_bytes=LIMIT),
        cost_estimate=pl.CostEstimate(flops=5 * 10**9, bytes_accessed=4 * 10**6, transcendentals=0),
        name="plan",
    )(*owns, *rest)


def correct_kernel(tile, *refs):
    raised_ref, x_hbm, own_ref = refs[:3]
    near_refs = refs[3:7]
    meta_ref, table_ref, place_ref, code_ref, fixed_ref = refs[7:12]
    pack_refs = refs[12:18]
    lifted_ref, payload_ref, total_ref, x_ref, sems = refs[18:]
    copies = fetches((x_hbm,), (x_ref,), sems)
    count = x_ref.shape[1]
    faces = own_ref.shape[2]
    cap = pack_refs[0].shape[1]
    table = face_table()

    def jumps(j, carry):
        lanes = pl.ds(pl.multiple_of(j * tile, tile), tile)
        for s in range(4):
            local = meta_ref[s, 1:2, lanes]
            pair = meta_ref[s, 2:3, lanes]
            orient = meta_ref[s, 3:4, lanes]
            matcher = match(faces, pair)
            paired = dot(near_refs[s][...], matcher)
            own = own_ref[s, :, lanes].astype(F32)
            jump = []
            for n in range(FMODES):
                best = paired[table[0][n] * FIELDS : (table[0][n] + 1) * FIELDS]
                for o in range(1, 6):
                    if table[o][n] != table[0][n]:
                        other = paired[table[o][n] * FIELDS : (table[o][n] + 1) * FIELDS]
                        best = jnp.where(orient == o, other, best)
                jump.append(0.5 * (best - own[n * FIELDS : (n + 1) * FIELDS]))
            jump = jnp.concatenate(jump, axis=0)
            split = jnp.concatenate([jnp.where(local == l, jump, 0.0) for l in range(4)], axis=0)
            lifted_ref[s, :, lanes] = dot(raised_ref[...], split.astype(BF16)).astype(BF16)
        return carry

    for s in range(4):
        lifted_ref[s, :, faces:] = jnp.zeros((ROWS, LANES), BF16)
    lax.fori_loop(0, faces // tile, jumps, 0)
    copies[0].wait()

    def fix(t, carry):
        at = pl.ds(pl.multiple_of(t * BUCKET, BUCKET), BUCKET)

        def window(s, i):
            begin = table_ref[8 * s + t, 0] + i * WINDOW
            lanes = pl.ds(pl.multiple_of(begin, LANES), WINDOW)
            return lifted_ref[s, :, lanes], match(BUCKET, meta_ref[s, 0:1, lanes] - t * BUCKET)

        both = [window(s, 0) for s in range(4)]
        total = x_ref[:, at].astype(F32) + lax.dot_general(
            jnp.concatenate([a for a, _ in both], axis=1),
            jnp.concatenate([b for _, b in both], axis=1),
            NT,
            preferred_element_type=F32,
        )
        total_ref[...] = total

        @pl.when(table_ref[t, 2] > 1)
        def _():
            for s in range(4):

                def more(i, carry, s=s):
                    a, b = window(s, i)
                    total_ref[...] += lax.dot_general(a, b, NT, preferred_element_type=F32)
                    return carry

                lax.fori_loop(1, table_ref[8 * s + t, 1], more, 0)

        total = total_ref[...]
        fixed_ref[:, at] = total.astype(BF16)
        code = jnp.broadcast_to(code_ref[:, at], (8, BUCKET)).astype(F32)
        payload_ref[:, at] = jnp.concatenate([total, code], axis=0).astype(BF16)
        return carry

    lax.fori_loop(0, count // BUCKET, fix, 0)
    for k, pack_ref in enumerate(pack_refs):
        packer = match(cap, place_ref[...] - k * cap)
        pack_ref[...] = lax.dot_general(
            payload_ref[...], packer, NT, preferred_element_type=F32
        ).astype(BF16)


def correct_call(x, own, near, meta, table, raised, place, code):
    count = x.shape[1]
    cap = count // 16
    faces = own.shape[2]
    rows = ROWS + 8
    return pl.pallas_call(
        functools.partial(correct_kernel, 512),
        in_specs=[VMEM_SPEC, HBM_SPEC] + [VMEM_SPEC] * 6 + [SMEM_SPEC] + [VMEM_SPEC] * 2,
        out_specs=[VMEM_SPEC] * 7,
        out_shape=[jax.ShapeDtypeStruct((ROWS, count), BF16)]
        + [jax.ShapeDtypeStruct((rows, cap), BF16)] * 6,
        scratch_shapes=[
            pltpu.VMEM((4, ROWS, faces + LANES), BF16),
            pltpu.VMEM((rows, count), BF16),
            pltpu.VMEM((ROWS, BUCKET), F32),
        ]
        + room(x),
        compiler_params=pltpu.CompilerParams(vmem_limit_bytes=LIMIT),
        cost_estimate=pl.CostEstimate(flops=10**10, bytes_accessed=10**7, transcendentals=0),
        name="correct",
    )(raised, x, own, *near, meta, table, place, code)


def joined_weights(prolong_ref):
    rows = []
    for c in range(2):
        total = jnp.zeros((PAD, 6 * PAD), F32)
        for e in range(6):
            left = ones_where(iota((PAD, MODES), 0) == iota((PAD, MODES), 1))
            right = ones_where(iota((MODES, 6 * PAD), 0) + e * PAD == iota((MODES, 6 * PAD), 1))
            total += dot(dot(left, prolong_ref[e, :, c, :]).astype(BF16), right)
        rows.append(total)
    return jnp.concatenate(rows, axis=0).astype(BF16)


def bisect_tile(weights, parents, state, wide_ref, kids_ref, put):
    chunks = state.shape[1] // LANES
    pieces = [slice(i * LANES, (i + 1) * LANES) for i in range(chunks)]
    parents = jnp.where(state >= 0, parents, 0.0)
    shape = (2 * PAD, state.shape[1])
    second = (iota(shape, 0) // PAD).astype(jnp.int16)
    cut = jnp.broadcast_to((state - 1).astype(jnp.int16), shape) - second
    for i, piece in enumerate(pieces):
        wide_ref[i, :ROWS, :] = parents[:, piece]
    for f in range(FIELDS):
        modes = jnp.concatenate(
            [wide_ref[i, pl.ds(f, PAD, stride=FIELDS), :] for i in range(chunks)], axis=1
        )
        twice = jnp.concatenate([modes, modes], axis=0).astype(BF16)
        masked = [jnp.where(cut == 2 * i, twice, jnp.array(0, BF16)) for i in range(3)]
        both = dot(weights, jnp.concatenate(masked, axis=0))
        for i, piece in enumerate(pieces):
            kids_ref[i, pl.ds(f, MODES, stride=FIELDS), :] = both[:MODES, piece]
            kids_ref[i, pl.ds(ROWS + f, MODES, stride=FIELDS), :] = both[PAD : PAD + MODES, piece]
    kids = jnp.concatenate([kids_ref[i] for i in range(chunks)], axis=1)
    put(0, jnp.where(state == 0, parents, kids[:ROWS]).astype(BF16))
    put(1, kids[ROWS:].astype(BF16))


def scratch_tiles():
    return [
        pltpu.VMEM((TILE // LANES, PAD * FIELDS, LANES), F32),
        pltpu.VMEM((TILE // LANES, 2 * ROWS, LANES), F32),
    ]


def clear(wide_ref):
    wide_ref[:, ROWS:, :] = jnp.zeros((TILE // LANES, PAD * FIELDS - ROWS, LANES), F32)


def home_kernel(fixed_ref, state_ref, prolong_ref, out_ref, weights_ref, wide_ref, kids_ref):
    t = pl.program_id(0)

    @pl.when(t == 0)
    def _():
        weights_ref[...] = joined_weights(prolong_ref)
        clear(wide_ref)

    at = pl.ds(pl.multiple_of(t * TILE, TILE), TILE)

    def put(child, value):
        out_ref[child] = value

    parents = fixed_ref[:, at].astype(F32)
    bisect_tile(weights_ref[...], parents, state_ref[:, at], wide_ref, kids_ref, put)


def home_call(fixed, state, prolong, slots):
    count = fixed.shape[1]
    return pl.pallas_call(
        home_kernel,
        grid=(count // TILE,),
        in_specs=[VMEM_SPEC, VMEM_SPEC, VMEM_SPEC],
        out_specs=[
            pl.BlockSpec((2, ROWS, TILE), lambda i: (0, 0, i)),
            pl.BlockSpec((2 * PAD, 6 * PAD), lambda i: (0, 0)),
        ],
        out_shape=[
            jax.ShapeDtypeStruct((2, ROWS, slots), BF16),
            jax.ShapeDtypeStruct((2 * PAD, 6 * PAD), BF16),
        ],
        scratch_shapes=scratch_tiles(),
        compiler_params=pltpu.CompilerParams(vmem_limit_bytes=LIMIT),
        cost_estimate=pl.CostEstimate(
            flops=2 * 560 * 280 * count, bytes_accessed=6 * ROWS * count, transcendentals=0
        ),
        name="home",
    )(fixed, state, prolong)


def incoming_kernel(*refs):
    parts, weights_ref, out_hbm = refs[:6], refs[6], refs[8]
    wide_ref, kids_ref, out_ref, sems = refs[9:]
    cap = parts[0].shape[1]
    first = out_hbm.shape[2] - 6 * cap
    clear(wide_ref)
    copies = []
    for k in range(3):
        block = jnp.concatenate([parts[2 * k][...], parts[2 * k + 1][...]], axis=1).astype(F32)
        state = block[ROWS : ROWS + 1].astype(jnp.int32)

        def put(child, value, k=k):
            out_ref[k, child] = value

        bisect_tile(weights_ref[...], block[:ROWS], state, wide_ref, kids_ref, put)
        target = out_hbm.at[:, :, pl.ds(first + k * TILE, TILE)]
        copies.append(pltpu.make_async_copy(out_ref.at[k], target, sems.at[k]))
        copies[-1].start()
    for copy in copies:
        copy.wait()


def incoming_call(parts, weights, kept):
    return pl.pallas_call(
        incoming_kernel,
        in_specs=[VMEM_SPEC] * 7 + [HBM_SPEC],
        out_specs=HBM_SPEC,
        out_shape=jax.ShapeDtypeStruct(kept.shape, BF16),
        scratch_shapes=scratch_tiles()
        + [pltpu.VMEM((3, 2, ROWS, TILE), BF16), pltpu.SemaphoreType.DMA((3,))],
        input_output_aliases={7: 0},
        compiler_params=pltpu.CompilerParams(vmem_limit_bytes=LIMIT),
        name="incoming",
    )(*parts, weights, kept)


def shards(
    parents,
    refine,
    edge,
    move,
    face_owner,
    face_local,
    face_pair,
    face_orient,
    prolong,
    restrict,
    lift,
):
    count = parents.shape[2]
    slots = count + 6 * (count // 16)
    x = parents.reshape(ROWS, count)
    prolong = prolong.transpose(0, 2, 1, 3)
    owns = trace_call(x, face_owner, face_local, restrict.transpose(1, 0, 2))
    span2 = passed_along(owns[3], "gz", 1)
    span3 = passed_along(owns[2], "gz", -1)
    stream0 = passed_along(owns[1], "gx", 1)
    stream1 = passed_along(owns[0], "gx", -1)
    near = [stream0, stream1, span2, span3]
    own, meta, table, raised, place, code, state = plan_call(
        owns,
        face_owner,
        face_local,
        face_pair,
        face_orient,
        lift.transpose(2, 0, 1),
        move[None, :],
        refine[None, :],
        edge[None, :],
    )
    fixed, *packs = correct_call(x, own, near, meta, table, raised, place, code)
    parts = [passed_along(packs[k], ("gx", "gz"), OFFSETS[k]) for k in range(6)]
    kept, weights = home_call(fixed, state, prolong, slots)
    out = incoming_call(parts, weights, kept)
    return out.reshape(2, MODES, FIELDS, slots)


def solution(mesh):
    whole = ("gx", "gz")
    side = P(None, whole, None)
    in_specs = (P(None, None, whole), P(whole), P(whole), P(whole), side, side, side, side, P(), P(), P())
    out_specs = P(None, None, None, whole)
    return jax.shard_map(shards, mesh=mesh, in_specs=in_specs, out_specs=out_specs, check_vma=False)
```

profile of v0, /device:TPU:6, one launch (start us, length us, event | category | flops | bytes accessed | tf_op | source)
XLA Modules:
  0.0 73.4 jit_solution(5359119536402763827)
XLA Ops:
  0.1 13.7 %trace.1 = (bf16[120,1024]{1,0:T(8,128)(2,1)S(1)}, bf16[120,1024]{1,0:T(8,128)(2,1)S(1)}, bf16[120,1024]{1,0:T(8,128)(2,1)S(1)}, bf16[120,1024]{1,0:T(8,128)(2,1)S(1)}) custom-call(bf16[15,4,35]{2,1,0:T(4,128)(2,1)} %bitcast.15, s32[4,1,1024]{2,1,0:T(1,128)} %refs_4_.1, s32[4,1,1024]{2,1,0:T(1,128)} %refs_5_.1, bf16[280,4096]{1,0:T(8,128)(2,1)} %bitcast.8), custom_call_target="tpu_custom_call" | custom-call | flops 10000000000 | bytes 10000000 | tf_op jit(solution)/shard_map/trace/pallas_call | solution.py:115
  13.8 6.0 %collective-permute-start.1 = (bf16[120,1024]{1,0:T(8,128)(2,1)S(1)}, bf16[120,1024]{1,0:T(8,128)(2,1)S(1)}, u32[]{:S(2)}, u32[]{:S(2)}) collective-permute-start(bf16[120,1024]{1,0:T(8,128)(2,1)S(1)} %get-tuple-element.25.refs_0_), channel_id=1, source_target_pairs={{4,0},{8,4},{12,8},{16,12},{20,16},{24,20},{28,24},{32,28},{36,32}... | collective-permute-start | bytes 737288 | tf_op jit(solution)/shard_map/ppermute | solution.py:29
  19.8 0.0 collective-permute-start
  19.8 0.8 %collective-permute-start.3 = (bf16[120,1024]{1,0:T(8,128)(2,1)S(1)}, bf16[120,1024]{1,0:T(8,128)(2,1)S(1)}, u32[]{:S(2)}, u32[]{:S(2)}) collective-permute-start(bf16[120,1024]{1,0:T(8,128)(2,1)S(1)} %get-tuple-element.27.refs_2_), channel_id=1, source_target_pairs={{1,0},{2,1},{3,2},{0,3},{5,4},{6,5},{7,6},{4,7},{9,8},{10,9},{11,1... | collective-permute-start | bytes 737288 | tf_op jit(solution)/shard_map/ppermute | solution.py:29
  20.6 2.4 %collective-permute-start.2 = (bf16[120,1024]{1,0:T(8,128)(2,1)S(1)}, bf16[120,1024]{1,0:T(8,128)(2,1)S(1)}, u32[]{:S(2)}, u32[]{:S(2)}) collective-permute-start(bf16[120,1024]{1,0:T(8,128)(2,1)S(1)} %get-tuple-element.28.refs_3_), channel_id=1, source_target_pairs={{3,0},{0,1},{1,2},{2,3},{7,4},{4,5},{5,6},{6,7},{11,8},{8,9},{9,10... | collective-permute-start | bytes 737288 | tf_op jit(solution)/shard_map/ppermute | solution.py:29
  23.1 0.0 copy-start
  23.1 4.1 %plan.1 = (bf16[4,120,1024]{2,1,0:T(8,128)(2,1)S(1)}, s32[4,8,1152]{2,1,0:T(8,128)S(1)}, s32[32,128]{1,0:T(8,128)S(1)}, bf16[280,480]{1,0:T(8,128)(2,1)S(1)}, s3...) custom-call(bf16[120,1024]{1,0:T(8,128)(2,1)S(1)} %get-tuple-element.25.refs_0_, ...), custom_call_target="tpu_custom_call" | custom-call | flops 5000000000 | bytes 4000000 | tf_op jit(solution)/shard_map/plan/pallas_call | solution.py:205
  27.2 1.5 %collective-permute-done.refs_3_ = bf16[120,1024]{1,0:T(8,128)(2,1)S(1)} collective-permute-done((bf16[120,1024]{1,0:T(8,128)(2,1)S(1)}, bf16[120,1024]{1,0:T(8,128)(2,1)S(1)}, u32[]{:S(2)}, u32[]{:S(2)}) %collective-permute-start) | collective-permute-done | bytes 245792 | tf_op jit(solution)/shard_map/ppermute | solution.py:29
  28.7 0.0 collective-permute-done.3.refs_6_
  28.8 0.0 collective-permute-done.2.refs_5_
  28.8 0.0 copy-start.1
  28.8 15.0 %correct.1 = (bf16[280,4096]{1,0:T(8,128)(2,1)S(1)}, bf16[288,256]{1,0:T(8,128)(2,1)S(1)}, bf16[288,256]{1,0:T(8,128)(2,1)S(1)}, bf16[288,256]{1,0:T(8,128)(2,1)...) custom-call(bf16[280,480]{1,0:T(8,128)(2,1)S(1)} %get-tuple-element.29.refs_0_, ...), custom_call_target="tpu_custom_call" | custom-call | flops 10000000000 | bytes 10000000 | tf_op jit(solution)/shard_map/correct/pallas_call | solution.py:311
  43.8 0.1 collective-permute-start.4
  43.9 0.1 collective-permute-start.5
  44.0 0.7 collective-permute-start.6
  44.7 2.3 %collective-permute-start.7 = (bf16[288,256]{1,0:T(8,128)(2,1)S(1)}, bf16[288,256]{1,0:T(8,128)(2,1)S(1)}, u32[]{:S(2)}, u32[]{:S(2)}) collective-permute-start(bf16[288,256]{1,0:T(8,128)(2,1)S(1)} %get-tuple-element.38), channel_id=1, source_target_pairs={{1,0},{2,1},{3,2},{4,3},{5,4},{6,5},{7,6},{8,7},{9,8},{10,9},{11,1... | collective-permute-start | bytes 442376 | tf_op jit(solution)/shard_map/ppermute | solution.py:29
  47.0 3.1 %collective-permute-start.8 = (bf16[288,256]{1,0:T(8,128)(2,1)S(1)}, bf16[288,256]{1,0:T(8,128)(2,1)S(1)}, u32[]{:S(2)}, u32[]{:S(2)}) collective-permute-start(bf16[288,256]{1,0:T(8,128)(2,1)S(1)} %get-tuple-element.39), channel_id=1, source_target_pairs={{2,0},{3,1},{4,2},{5,3},{6,4},{7,5},{8,6},{9,7},{10,8},{11,9},{12,... | collective-permute-start | bytes 442376 | tf_op jit(solution)/shard_map/ppermute | solution.py:29
  50.0 2.4 %collective-permute-done.4.refs_0_ = bf16[288,256]{1,0:T(8,128)(2,1)S(1)} collective-permute-done((bf16[288,256]{1,0:T(8,128)(2,1)S(1)}, bf16[288,256]{1,0:T(8,128)(2,1)S(1)}, u32[]{:S(2)}, u32[]{:S(2)}) %collective-permute-start.4) | collective-permute-done | bytes 147488 | tf_op jit(solution)/shard_map/ppermute | solution.py:29
  52.5 10.3 %collective-permute-start.9 = (bf16[288,256]{1,0:T(8,128)(2,1)S(1)}, bf16[288,256]{1,0:T(8,128)(2,1)S(1)}, u32[]{:S(2)}, u32[]{:S(2)}) collective-permute-start(bf16[288,256]{1,0:T(8,128)(2,1)S(1)} %get-tuple-element.40), channel_id=1, source_target_pairs={{3,0},{4,1},{5,2},{6,3},{7,4},{8,5},{9,6},{10,7},{11,8},{12,9},{13... | collective-permute-start | bytes 442376 | tf_op jit(solution)/shard_map/ppermute | solution.py:29
  62.8 7.6 %home.1 = (bf16[2,280,5632]{2,1,0:T(8,128)(2,1)}, bf16[80,240]{1,0:T(8,128)(2,1)S(1)}) custom-call(bf16[280,4096]{1,0:T(8,128)(2,1)S(1)} %get-tuple-element.41.fixed_ref, s32[1,4096]{1,0:T(1,128)S(1)} %get-tuple-element.42.state_ref, bf16[6,35,2,35]{3,2,1,0:T(2,128)(2,1)S(1)} %bitcast.10), custom_call_target="tpu_custom_call" | custom-call | flops 1284505600 | bytes 6881280 | tf_op jit(solution)/shard_map/home/pallas_call | solution.py:395
  70.4 0.0 collective-permute-done.5.refs_1_
  70.4 0.0 collective-permute-done.6.refs_2_
  70.4 0.0 collective-permute-done.8.refs_4_
  70.4 2.8 %incoming.1 = bf16[2,280,5632]{2,1,0:T(8,128)(2,1)} custom-call(bf16[288,256]{1,0:T(8,128)(2,1)S(1)} %collective-permute-done.4.refs_0_, bf16[288,256]{1,0:T(8,128)(2,1)S(1)} %collective-permute-done.5.refs_1_, bf16[288,256]{1,0:T(8,128)(2,1)S(1)} %collective-permute-done.6.refs_2_, ...), custom_call_target="tpu_custom_call", output_to_operand_aliasing={{}: (7, {})} | custom-call | tf_op jit(solution)/shard_map/incoming/pallas_call | solution.py:439
  (21 shorter events, 0.0 us)
Async XLA Ops:
  0.0 23.0 %copy-start.2 = (f32[4,35,15]{1,0,2:T(4,128)S(1)}, f32[4,35,15]{1,0,2:T(4,128)}, u32[]{:S(2)}) copy-start(f32[4,35,15]{1,0,2:T(4,128)} %param.21) | copy-start | bytes 25204
  0.0 23.0 %copy-start.3 = (s32[4,1,1024]{2,1,0:T(1,128)S(1)}, s32[4,1,1024]{2,1,0:T(1,128)}, u32[]{:S(2)}) copy-start(s32[4,1,1024]{2,1,0:T(1,128)} %refs_4_.1) | copy-start | bytes 49156
  0.0 23.0 %copy-start.4 = (s32[4,1,1024]{2,1,0:T(1,128)S(1)}, s32[4,1,1024]{2,1,0:T(1,128)}, u32[]{:S(2)}) copy-start(s32[4,1,1024]{2,1,0:T(1,128)} %refs_5_.1) | copy-start | bytes 49156
  0.0 23.0 %copy-start.5 = (s32[4,1,1024]{2,1,0:T(1,128)S(1)}, s32[4,1,1024]{2,1,0:T(1,128)}, u32[]{:S(2)}) copy-start(s32[4,1,1024]{2,1,0:T(1,128)} %refs_6_.1) | copy-start | bytes 49156
  0.0 23.0 %copy-start.6 = (s32[4,1,1024]{2,1,0:T(1,128)S(1)}, s32[4,1,1024]{2,1,0:T(1,128)}, u32[]{:S(2)}) copy-start(s32[4,1,1024]{2,1,0:T(1,128)} %refs_7_.1) | copy-start | bytes 49156
  0.0 23.0 %copy-start.7 = (s32[4096]{0:T(1024)S(1)}, s32[4096]{0:T(1024)}, u32[]{:S(2)}) copy-start(s32[4096]{0:T(1024)} %param.14) | copy-start | bytes 49156
  0.0 23.0 %copy-start.8 = (s32[4096]{0:T(1024)S(1)}, s32[4096]{0:T(1024)}, u32[]{:S(2)}) copy-start(s32[4096]{0:T(1024)} %param.12) | copy-start | bytes 49156
  0.0 23.0 %copy-start.9 = (s32[4096]{0:T(1024)S(1)}, s32[4096]{0:T(1024)}, u32[]{:S(2)}) copy-start(s32[4096]{0:T(1024)} %param.13) | copy-start | bytes 49156
  13.8 13.4 %collective-permute-start.1 = (bf16[120,1024]{1,0:T(8,128)(2,1)S(1)}, bf16[120,1024]{1,0:T(8,128)(2,1)S(1)}, u32[]{:S(2)}, u32[]{:S(2)}) collective-permute-start(bf16[120,1024]{1,0:T(8,128)(2,1)S(1)} %get-tuple-element.25.refs_0_), channel_id=1, source_target_pairs={{4,0},{8,4},{12,8},{16,12},{20,16},{24,20},{28,24},{32,28},{36,32}... | collective-permute-start | bytes 737288 | tf_op jit(solution)/shard_map/ppermute | solution.py:29
  19.8 8.9 %collective-permute-start = (bf16[120,1024]{1,0:T(8,128)(2,1)S(1)}, bf16[120,1024]{1,0:T(8,128)(2,1)S(1)}, u32[]{:S(2)}, u32[]{:S(2)}) collective-permute-start(bf16[120,1024]{1,0:T(8,128)(2,1)S(1)} %get-tuple-element.26.refs_1_), channel_id=1, source_target_pairs={{124,0},{0,4},{4,8},{8,12},{12,16},{16,20},{20,24},{24,28},{28,32}... | collective-permute-start | bytes 737288 | tf_op jit(solution)/shard_map/ppermute | solution.py:29
  19.8 8.9 %collective-permute-start.3 = (bf16[120,1024]{1,0:T(8,128)(2,1)S(1)}, bf16[120,1024]{1,0:T(8,128)(2,1)S(1)}, u32[]{:S(2)}, u32[]{:S(2)}) collective-permute-start(bf16[120,1024]{1,0:T(8,128)(2,1)S(1)} %get-tuple-element.27.refs_2_), channel_id=1, source_target_pairs={{1,0},{2,1},{3,2},{0,3},{5,4},{6,5},{7,6},{4,7},{9,8},{10,9},{11,1... | collective-permute-start | bytes 737288 | tf_op jit(solution)/shard_map/ppermute | solution.py:29
  20.6 8.1 %collective-permute-start.2 = (bf16[120,1024]{1,0:T(8,128)(2,1)S(1)}, bf16[120,1024]{1,0:T(8,128)(2,1)S(1)}, u32[]{:S(2)}, u32[]{:S(2)}) collective-permute-start(bf16[120,1024]{1,0:T(8,128)(2,1)S(1)} %get-tuple-element.28.refs_3_), channel_id=1, source_target_pairs={{3,0},{0,1},{1,2},{2,3},{7,4},{4,5},{5,6},{6,7},{11,8},{8,9},{9,10... | collective-permute-start | bytes 737288 | tf_op jit(solution)/shard_map/ppermute | solution.py:29
  23.1 5.7 %copy-start = (bf16[35,8,4096]{2,1,0:T(8,128)(2,1)S(1)}, bf16[35,8,4096]{2,1,0:T(8,128)(2,1)}, u32[]{:S(2)}) copy-start(bf16[35,8,4096]{2,1,0:T(8,128)(2,1)} %param.11) | copy-start | bytes 6881284
  28.8 34.1 %copy-start.1 = (bf16[6,2,35,35]{3,1,2,0:T(2,128)(2,1)S(1)}, bf16[6,2,35,35]{3,1,2,0:T(2,128)(2,1)}, u32[]{:S(2)}) copy-start(bf16[6,2,35,35]{3,1,2,0:T(2,128)(2,1)} %param.19) | copy-start | bytes 88204
  43.8 8.7 %collective-permute-start.4 = (bf16[288,256]{1,0:T(8,128)(2,1)S(1)}, bf16[288,256]{1,0:T(8,128)(2,1)S(1)}, u32[]{:S(2)}, u32[]{:S(2)}) collective-permute-start(bf16[288,256]{1,0:T(8,128)(2,1)S(1)} %get-tuple-element.35), channel_id=1, source_target_pairs={{127,0},{0,1},{1,2},{2,3},{3,4},{4,5},{5,6},{6,7},{7,8},{8,9},{9,1... | collective-permute-start | bytes 442376 | tf_op jit(solution)/shard_map/ppermute | solution.py:29
  43.9 26.5 %collective-permute-start.5 = (bf16[288,256]{1,0:T(8,128)(2,1)S(1)}, bf16[288,256]{1,0:T(8,128)(2,1)S(1)}, u32[]{:S(2)}, u32[]{:S(2)}) collective-permute-start(bf16[288,256]{1,0:T(8,128)(2,1)S(1)} %get-tuple-element.36), channel_id=1, source_target_pairs={{126,0},{127,1},{0,2},{1,3},{2,4},{3,5},{4,6},{5,7},{6,8},{7,9},{8... | collective-permute-start | bytes 442376 | tf_op jit(solution)/shard_map/ppermute | solution.py:29
  44.0 26.4 %collective-permute-start.6 = (bf16[288,256]{1,0:T(8,128)(2,1)S(1)}, bf16[288,256]{1,0:T(8,128)(2,1)S(1)}, u32[]{:S(2)}, u32[]{:S(2)}) collective-permute-start(bf16[288,256]{1,0:T(8,128)(2,1)S(1)} %get-tuple-element.37), channel_id=1, source_target_pairs={{125,0},{126,1},{127,2},{0,3},{1,4},{2,5},{3,6},{4,7},{5,8},{6,9},... | collective-permute-start | bytes 442376 | tf_op jit(solution)/shard_map/ppermute | solution.py:29
  44.7 25.7 %collective-permute-start.7 = (bf16[288,256]{1,0:T(8,128)(2,1)S(1)}, bf16[288,256]{1,0:T(8,128)(2,1)S(1)}, u32[]{:S(2)}, u32[]{:S(2)}) collective-permute-start(bf16[288,256]{1,0:T(8,128)(2,1)S(1)} %get-tuple-element.38), channel_id=1, source_target_pairs={{1,0},{2,1},{3,2},{4,3},{5,4},{6,5},{7,6},{8,7},{9,8},{10,9},{11,1... | collective-permute-start | bytes 442376 | tf_op jit(solution)/shard_map/ppermute | solution.py:29
  47.0 23.5 %collective-permute-start.8 = (bf16[288,256]{1,0:T(8,128)(2,1)S(1)}, bf16[288,256]{1,0:T(8,128)(2,1)S(1)}, u32[]{:S(2)}, u32[]{:S(2)}) collective-permute-start(bf16[288,256]{1,0:T(8,128)(2,1)S(1)} %get-tuple-element.39), channel_id=1, source_target_pairs={{2,0},{3,1},{4,2},{5,3},{6,4},{7,5},{8,6},{9,7},{10,8},{11,9},{12,... | collective-permute-start | bytes 442376 | tf_op jit(solution)/shard_map/ppermute | solution.py:29
  52.5 18.0 %collective-permute-start.9 = (bf16[288,256]{1,0:T(8,128)(2,1)S(1)}, bf16[288,256]{1,0:T(8,128)(2,1)S(1)}, u32[]{:S(2)}, u32[]{:S(2)}) collective-permute-start(bf16[288,256]{1,0:T(8,128)(2,1)S(1)} %get-tuple-element.40), channel_id=1, source_target_pairs={{3,0},{4,1},{5,2},{6,3},{7,4},{8,5},{9,6},{10,7},{11,8},{12,9},{13... | collective-permute-start | bytes 442376 | tf_op jit(solution)/shard_map/ppermute | solution.py:29
where the time goes:
time: 73.6 us; the launch traced here: 73.4 us
  Pallas kernels  43.2 us (59%)
  starting transfers between devices  25.8 us (35%)
  waiting for transfers between devices  4.01 us (5%)
    ppermute x10, starting transfers between devices, passed_along(): lax.ppermute(block, axis, [((i - distance) % count, i) for i in range(cou...  25.8 us
    pallas_call x1, Pallas kernels, correct_call(): pl.pallas_call(functools.partial(correct_kernel, 512), in_specs=[VMEM_SPE...  15 us
    pallas_call x1, Pallas kernels, trace_call(): pl.pallas_call(functools.partial(trace_kernel, 1024), in_specs=[HBM_SPEC]...  13.7 us
    pallas_call x1, Pallas kernels, home_call(): pl.pallas_call(home_kernel, grid=(count // TILE,), in_specs=[VMEM_SPEC, V...  7.59 us
    pallas_call x1, Pallas kernels, plan_call(): pl.pallas_call(plan_kernel, in_specs=[VMEM_SPEC] * 4 + [HBM_SPEC] * 8, ou...  4.07 us
    ppermute x10, waiting for transfers between devices, passed_along(): lax.ppermute(block, axis, [((i - distance) % count, i) for i in range(cou...  4.01 us
    pallas_call x1, Pallas kernels, incoming_call(): pl.pallas_call(incoming_kernel, in_specs=[VMEM_SPEC] * 7 + [HBM_SPEC], ou...  2.8 us
  transfers between devices with their start and end apart: 10, of which 2 were waited for; matrix products, arithmetic and copies ran while one was open for 0% of the time, Pallas kernels for 16%

commit v1 on v0

--- a/solution.py
+++ b/solution.py
@@ -16,7 +16,8 @@
 LANES = 128
 BUCKET = 512
 WINDOW = 256
-TILE = 512
+PART = 256
+SETS = 4
 LIMIT = 30 << 20
 OFFSETS = (1, 2, 3, -1, -2, -3)
 F32 = jnp.float32
@@ -338,73 +339,74 @@
     return jnp.concatenate(rows, axis=0).astype(BF16)
 
 
-def bisect_tile(weights, parents, state, wide_ref, kids_ref, put):
-    chunks = state.shape[1] // LANES
-    pieces = [slice(i * LANES, (i + 1) * LANES) for i in range(chunks)]
+def bisect_part(weights, parents, state, wide_ref, kids_ref, put):
+    pieces = [slice(i * LANES, (i + 1) * LANES) for i in range(PART // LANES)]
     parents = jnp.where(state >= 0, parents, 0.0)
-    shape = (2 * PAD, state.shape[1])
+    shape = (2 * PAD, PART)
     second = (iota(shape, 0) // PAD).astype(jnp.int16)
     cut = jnp.broadcast_to((state - 1).astype(jnp.int16), shape) - second
     for i, piece in enumerate(pieces):
         wide_ref[i, :ROWS, :] = parents[:, piece]
     for f in range(FIELDS):
-        modes = jnp.concatenate(
-            [wide_ref[i, pl.ds(f, PAD, stride=FIELDS), :] for i in range(chunks)], axis=1
-        )
+        modes = [wide_ref[i, pl.ds(f, PAD, stride=FIELDS), :] for i in range(len(pieces))]
+        modes = jnp.concatenate(modes, axis=1)
         twice = jnp.concatenate([modes, modes], axis=0).astype(BF16)
         masked = [jnp.where(cut == 2 * i, twice, jnp.array(0, BF16)) for i in range(3)]
         both = dot(weights, jnp.concatenate(masked, axis=0))
         for i, piece in enumerate(pieces):
             kids_ref[i, pl.ds(f, MODES, stride=FIELDS), :] = both[:MODES, piece]
             kids_ref[i, pl.ds(ROWS + f, MODES, stride=FIELDS), :] = both[PAD : PAD + MODES, piece]
-    kids = jnp.concatenate([kids_ref[i] for i in range(chunks)], axis=1)
+    kids = jnp.concatenate([kids_ref[i] for i in range(len(pieces))], axis=1)
     put(0, jnp.where(state == 0, parents, kids[:ROWS]).astype(BF16))
     put(1, kids[ROWS:].astype(BF16))
 
 
-def scratch_tiles():
-    return [
-        pltpu.VMEM((TILE // LANES, PAD * FIELDS, LANES), F32),
-        pltpu.VMEM((TILE // LANES, 2 * ROWS, LANES), F32),
-    ]
-
-
-def clear(wide_ref):
-    wide_ref[:, ROWS:, :] = jnp.zeros((TILE // LANES, PAD * FIELDS - ROWS, LANES), F32)
-
-
-def home_kernel(fixed_ref, state_ref, prolong_ref, out_ref, weights_ref, wide_ref, kids_ref):
+def scratch_sets():
+    wide = pltpu.VMEM((PART // LANES, PAD * FIELDS, LANES), F32)
+    kids = pltpu.VMEM((PART // LANES, 2 * ROWS, LANES), F32)
+    return [wide] * SETS + [kids] * SETS
+
+
+def clear(wide_refs):
+    for wide_ref in wide_refs:
+        wide_ref[:, ROWS:, :] = jnp.zeros((PART // LANES, PAD * FIELDS - ROWS, LANES), F32)
+
+
+def home_kernel(fixed_ref, state_ref, prolong_ref, out_ref, weights_ref, *scratch):
+    wide_refs, kids_refs = scratch[:SETS], scratch[SETS:]
     t = pl.program_id(0)
 
     @pl.when(t == 0)
     def _():
         weights_ref[...] = joined_weights(prolong_ref)
-        clear(wide_ref)
-
-    at = pl.ds(pl.multiple_of(t * TILE, TILE), TILE)
-
-    def put(child, value):
-        out_ref[child] = value
-
-    parents = fixed_ref[:, at].astype(F32)
-    bisect_tile(weights_ref[...], parents, state_ref[:, at], wide_ref, kids_ref, put)
+        clear(wide_refs)
+
+    for h in range(SETS):
+        at = pl.ds(pl.multiple_of(t * (SETS * PART) + h * PART, PART), PART)
+
+        def put(child, value, h=h):
+            out_ref[child, :, h * PART : (h + 1) * PART] = value
+
+        parents = fixed_ref[:, at].astype(F32)
+        bisect_part(weights_ref[...], parents, state_ref[:, at], wide_refs[h], kids_refs[h], put)
 
 
 def home_call(fixed, state, prolong, slots):
     count = fixed.shape[1]
+    tile = SETS * PART
     return pl.pallas_call(
         home_kernel,
-        grid=(count // TILE,),
+        grid=(count // tile,),
         in_specs=[VMEM_SPEC, VMEM_SPEC, VMEM_SPEC],
         out_specs=[
-            pl.BlockSpec((2, ROWS, TILE), lambda i: (0, 0, i)),
+            pl.BlockSpec((2, ROWS, tile), lambda i: (0, 0, i)),
             pl.BlockSpec((2 * PAD, 6 * PAD), lambda i: (0, 0)),
         ],
         out_shape=[
             jax.ShapeDtypeStruct((2, ROWS, slots), BF16),
             jax.ShapeDtypeStruct((2 * PAD, 6 * PAD), BF16),
         ],
-        scratch_shapes=scratch_tiles(),
+        scratch_shapes=scratch_sets(),
         compiler_params=pltpu.CompilerParams(vmem_limit_bytes=LIMIT),
         cost_estimate=pl.CostEstimate(
             flops=2 * 560 * 280 * count, bytes_accessed=6 * ROWS * count, transcendentals=0
@@ -415,20 +417,22 @@
 
 def incoming_kernel(*refs):
     parts, weights_ref, out_hbm = refs[:6], refs[6], refs[8]
-    wide_ref, kids_ref, out_ref, sems = refs[9:]
+    wide_refs, kids_refs = refs[9 : 9 + SETS], refs[9 + SETS : 9 + 2 * SETS]
+    out_ref, sems = refs[9 + 2 * SETS :]
     cap = parts[0].shape[1]
     first = out_hbm.shape[2] - 6 * cap
-    clear(wide_ref)
+    clear(wide_refs)
     copies = []
-    for k in range(3):
-        block = jnp.concatenate([parts[2 * k][...], parts[2 * k + 1][...]], axis=1).astype(F32)
+    for k in range(6):
+        block = parts[k][...].astype(F32)
         state = block[ROWS : ROWS + 1].astype(jnp.int32)
 
         def put(child, value, k=k):
             out_ref[k, child] = value
 
-        bisect_tile(weights_ref[...], block[:ROWS], state, wide_ref, kids_ref, put)
-        target = out_hbm.at[:, :, pl.ds(first + k * TILE, TILE)]
+        h = k % SETS
+        bisect_part(weights_ref[...], block[:ROWS], state, wide_refs[h], kids_refs[h], put)
+        target = out_hbm.at[:, :, pl.ds(first + k * cap, cap)]
         copies.append(pltpu.make_async_copy(out_ref.at[k], target, sems.at[k]))
         copies[-1].start()
     for copy in copies:
@@ -441,8 +445,8 @@
         in_specs=[VMEM_SPEC] * 7 + [HBM_SPEC],
         out_specs=HBM_SPEC,
         out_shape=jax.ShapeDtypeStruct(kept.shape, BF16),
-        scratch_shapes=scratch_tiles()
-        + [pltpu.VMEM((3, 2, ROWS, TILE), BF16), pltpu.SemaphoreType.DMA((3,))],
+        scratch_shapes=scratch_sets()
+        + [pltpu.VMEM((6, 2, ROWS, PART), BF16), pltpu.SemaphoreType.DMA((6,))],
         input_output_aliases={7: 0},
         compiler_params=pltpu.CompilerParams(vmem_limit_bytes=LIMIT),
         name="incoming",

time: 73.6 us -> 72 us (0.978)
  Pallas kernels: 43.2 us -> 41.7 us
    pallas_call x1, Pallas kernels: 7.59 us -> 6.49 us  [home_call(): pl.pallas_call(home_kernel, grid=(count // tile,), in_specs=[VMEM_SPEC, V...]
  transfers between devices with their start and end apart: 10 -> 10, of which waited for: 2 -> 2; matrix products, arithmetic and copies ran while one was open for 0% -> 0% of each run, Pallas kernels for 16% -> 15%
where the time goes in v1:
time: 72 us; the launch traced here: 71.9 us
  Pallas kernels  41.7 us (58%)
  starting transfers between devices  25.8 us (36%)
  waiting for transfers between devices  4.01 us (6%)
    ppermute x10, starting transfers between devices, passed_along(): lax.ppermute(block, axis, [((i - distance) % count, i) for i in range(cou...  25.8 us
    pallas_call x1, Pallas kernels, correct_call(): pl.pallas_call(functools.partial(correct_kernel, 512), in_specs=[VMEM_SPE...  15 us
    pallas_call x1, Pallas kernels, trace_call(): pl.pallas_call(functools.partial(trace_kernel, 1024), in_specs=[HBM_SPEC]...  13.7 us
    pallas_call x1, Pallas kernels, home_call(): pl.pallas_call(home_kernel, grid=(count // tile,), in_specs=[VMEM_SPEC, V...  6.49 us
    pallas_call x1, Pallas kernels, plan_call(): pl.pallas_call(plan_kernel, in_specs=[VMEM_SPEC] * 4 + [HBM_SPEC] * 8, ou...  4.07 us
    ppermute x10, waiting for transfers between devices, passed_along(): lax.ppermute(block, axis, [((i - distance) % count, i) for i in range(cou...  4.01 us
    pallas_call x1, Pallas kernels, incoming_call(): pl.pallas_call(incoming_kernel, in_specs=[VMEM_SPEC] * 7 + [HBM_SPEC], ou...  2.39 us
  transfers between devices with their start and end apart: 10, of which 2 were waited for; matrix products, arithmetic and copies ran while one was open for 0% of the time, Pallas kernels for 15%

profile of v1, /device:TPU:6, one launch (start us, length us, event | category | flops | bytes accessed | tf_op | source)
XLA Modules:
  0.0 71.9 jit_solution(5972509971664774781)
XLA Ops:
  0.1 13.7 %trace.1 = (bf16[120,1024]{1,0:T(8,128)(2,1)S(1)}, bf16[120,1024]{1,0:T(8,128)(2,1)S(1)}, bf16[120,1024]{1,0:T(8,128)(2,1)S(1)}, bf16[120,1024]{1,0:T(8,128)(2,1)S(1)}) custom-call(bf16[15,4,35]{2,1,0:T(4,128)(2,1)} %bitcast.15, s32[4,1,1024]{2,1,0:T(1,128)} %refs_4_.1, s32[4,1,1024]{2,1,0:T(1,128)} %refs_5_.1, bf16[280,4096]{1,0:T(8,128)(2,1)} %bitcast.8), custom_call_target="tpu_custom_call" | custom-call | flops 10000000000 | bytes 10000000 | tf_op jit(solution)/shard_map/trace/pallas_call | solution.py:116
  13.8 6.0 %collective-permute-start.1 = (bf16[120,1024]{1,0:T(8,128)(2,1)S(1)}, bf16[120,1024]{1,0:T(8,128)(2,1)S(1)}, u32[]{:S(2)}, u32[]{:S(2)}) collective-permute-start(bf16[120,1024]{1,0:T(8,128)(2,1)S(1)} %get-tuple-element.25.refs_0_), channel_id=1, source_target_pairs={{4,0},{8,4},{12,8},{16,12},{20,16},{24,20},{28,24},{32,28},{36,32}... | collective-permute-start | bytes 737288 | tf_op jit(solution)/shard_map/ppermute | solution.py:30
  19.8 0.0 collective-permute-start
  19.8 0.8 %collective-permute-start.3 = (bf16[120,1024]{1,0:T(8,128)(2,1)S(1)}, bf16[120,1024]{1,0:T(8,128)(2,1)S(1)}, u32[]{:S(2)}, u32[]{:S(2)}) collective-permute-start(bf16[120,1024]{1,0:T(8,128)(2,1)S(1)} %get-tuple-element.27.refs_2_), channel_id=1, source_target_pairs={{1,0},{2,1},{3,2},{0,3},{5,4},{6,5},{7,6},{4,7},{9,8},{10,9},{11,1... | collective-permute-start | bytes 737288 | tf_op jit(solution)/shard_map/ppermute | solution.py:30
  20.6 2.4 %collective-permute-start.2 = (bf16[120,1024]{1,0:T(8,128)(2,1)S(1)}, bf16[120,1024]{1,0:T(8,128)(2,1)S(1)}, u32[]{:S(2)}, u32[]{:S(2)}) collective-permute-start(bf16[120,1024]{1,0:T(8,128)(2,1)S(1)} %get-tuple-element.28.refs_3_), channel_id=1, source_target_pairs={{3,0},{0,1},{1,2},{2,3},{7,4},{4,5},{5,6},{6,7},{11,8},{8,9},{9,10... | collective-permute-start | bytes 737288 | tf_op jit(solution)/shard_map/ppermute | solution.py:30
  23.1 0.0 copy-start
  23.1 4.1 %plan.1 = (bf16[4,120,1024]{2,1,0:T(8,128)(2,1)S(1)}, s32[4,8,1152]{2,1,0:T(8,128)S(1)}, s32[32,128]{1,0:T(8,128)S(1)}, bf16[280,480]{1,0:T(8,128)(2,1)S(1)}, s3...) custom-call(bf16[120,1024]{1,0:T(8,128)(2,1)S(1)} %get-tuple-element.25.refs_0_, ...), custom_call_target="tpu_custom_call" | custom-call | flops 5000000000 | bytes 4000000 | tf_op jit(solution)/shard_map/plan/pallas_call | solution.py:206
  27.2 1.5 %collective-permute-done.refs_3_ = bf16[120,1024]{1,0:T(8,128)(2,1)S(1)} collective-permute-done((bf16[120,1024]{1,0:T(8,128)(2,1)S(1)}, bf16[120,1024]{1,0:T(8,128)(2,1)S(1)}, u32[]{:S(2)}, u32[]{:S(2)}) %collective-permute-start) | collective-permute-done | bytes 245792 | tf_op jit(solution)/shard_map/ppermute | solution.py:30
  28.7 0.0 collective-permute-done.3.refs_6_
  28.8 0.0 collective-permute-done.2.refs_5_
  28.8 0.0 copy-start.1
  28.8 15.0 %correct.1 = (bf16[280,4096]{1,0:T(8,128)(2,1)S(1)}, bf16[288,256]{1,0:T(8,128)(2,1)S(1)}, bf16[288,256]{1,0:T(8,128)(2,1)S(1)}, bf16[288,256]{1,0:T(8,128)(2,1)...) custom-call(bf16[280,480]{1,0:T(8,128)(2,1)S(1)} %get-tuple-element.29.refs_0_, ...), custom_call_target="tpu_custom_call" | custom-call | flops 10000000000 | bytes 10000000 | tf_op jit(solution)/shard_map/correct/pallas_call | solution.py:312
  43.8 0.1 collective-permute-start.4
  43.9 0.1 collective-permute-start.5
  44.0 0.7 %collective-permute-start.6 = (bf16[288,256]{1,0:T(8,128)(2,1)S(1)}, bf16[288,256]{1,0:T(8,128)(2,1)S(1)}, u32[]{:S(2)}, u32[]{:S(2)}) collective-permute-start(bf16[288,256]{1,0:T(8,128)(2,1)S(1)} %get-tuple-element.37), channel_id=1, source_target_pairs={{125,0},{126,1},{127,2},{0,3},{1,4},{2,5},{3,6},{4,7},{5,8},{6,9},... | collective-permute-start | bytes 442376 | tf_op jit(solution)/shard_map/ppermute | solution.py:30
  44.7 2.3 %collective-permute-start.7 = (bf16[288,256]{1,0:T(8,128)(2,1)S(1)}, bf16[288,256]{1,0:T(8,128)(2,1)S(1)}, u32[]{:S(2)}, u32[]{:S(2)}) collective-permute-start(bf16[288,256]{1,0:T(8,128)(2,1)S(1)} %get-tuple-element.38), channel_id=1, source_target_pairs={{1,0},{2,1},{3,2},{4,3},{5,4},{6,5},{7,6},{8,7},{9,8},{10,9},{11,1... | collective-permute-start | bytes 442376 | tf_op jit(solution)/shard_map/ppermute | solution.py:30
  47.0 3.1 %collective-permute-start.8 = (bf16[288,256]{1,0:T(8,128)(2,1)S(1)}, bf16[288,256]{1,0:T(8,128)(2,1)S(1)}, u32[]{:S(2)}, u32[]{:S(2)}) collective-permute-start(bf16[288,256]{1,0:T(8,128)(2,1)S(1)} %get-tuple-element.39), channel_id=1, source_target_pairs={{2,0},{3,1},{4,2},{5,3},{6,4},{7,5},{8,6},{9,7},{10,8},{11,9},{12,... | collective-permute-start | bytes 442376 | tf_op jit(solution)/shard_map/ppermute | solution.py:30
  50.0 2.4 %collective-permute-done.4.refs_0_ = bf16[288,256]{1,0:T(8,128)(2,1)S(1)} collective-permute-done((bf16[288,256]{1,0:T(8,128)(2,1)S(1)}, bf16[288,256]{1,0:T(8,128)(2,1)S(1)}, u32[]{:S(2)}, u32[]{:S(2)}) %collective-permute-start.4) | collective-permute-done | bytes 147488 | tf_op jit(solution)/shard_map/ppermute | solution.py:30
  52.5 10.3 %collective-permute-start.9 = (bf16[288,256]{1,0:T(8,128)(2,1)S(1)}, bf16[288,256]{1,0:T(8,128)(2,1)S(1)}, u32[]{:S(2)}, u32[]{:S(2)}) collective-permute-start(bf16[288,256]{1,0:T(8,128)(2,1)S(1)} %get-tuple-element.40), channel_id=1, source_target_pairs={{3,0},{4,1},{5,2},{6,3},{7,4},{8,5},{9,6},{10,7},{11,8},{12,9},{13... | collective-permute-start | bytes 442376 | tf_op jit(solution)/shard_map/ppermute | solution.py:30
  62.8 6.5 %home.1 = (bf16[2,280,5632]{2,1,0:T(8,128)(2,1)}, bf16[80,240]{1,0:T(8,128)(2,1)S(1)}) custom-call(bf16[280,4096]{1,0:T(8,128)(2,1)S(1)} %get-tuple-element.41.fixed_ref, s32[1,4096]{1,0:T(1,128)S(1)} %get-tuple-element.42.state_ref, bf16[6,35,2,35]{3,2,1,0:T(2,128)(2,1)S(1)} %bitcast.10), custom_call_target="tpu_custom_call" | custom-call | flops 1284505600 | bytes 6881280 | tf_op jit(solution)/shard_map/home/pallas_call | solution.py:397
  69.3 0.0 collective-permute-done.5.refs_1_
  69.3 0.0 collective-permute-done.6.refs_2_
  69.3 0.0 collective-permute-done.7.refs_3_
  69.3 2.4 %incoming.1 = bf16[2,280,5632]{2,1,0:T(8,128)(2,1)} custom-call(bf16[288,256]{1,0:T(8,128)(2,1)S(1)} %collective-permute-done.4.refs_0_, bf16[288,256]{1,0:T(8,128)(2,1)S(1)} %collective-permute-done.5.refs_1_, bf16[288,256]{1,0:T(8,128)(2,1)S(1)} %collective-permute-done.6.refs_2_, ...), custom_call_target="tpu_custom_call", output_to_operand_aliasing={{}: (7, {})} | custom-call | tf_op jit(solution)/shard_map/incoming/pallas_call | solution.py:443
  (21 shorter events, 0.0 us)
Async XLA Ops:
  0.0 23.0 %copy-start.2 = (f32[4,35,15]{1,0,2:T(4,128)S(1)}, f32[4,35,15]{1,0,2:T(4,128)}, u32[]{:S(2)}) copy-start(f32[4,35,15]{1,0,2:T(4,128)} %param.21) | copy-start | bytes 25204
  0.0 23.0 %copy-start.3 = (s32[4,1,1024]{2,1,0:T(1,128)S(1)}, s32[4,1,1024]{2,1,0:T(1,128)}, u32[]{:S(2)}) copy-start(s32[4,1,1024]{2,1,0:T(1,128)} %refs_4_.1) | copy-start | bytes 49156
  0.0 23.0 %copy-start.4 = (s32[4,1,1024]{2,1,0:T(1,128)S(1)}, s32[4,1,1024]{2,1,0:T(1,128)}, u32[]{:S(2)}) copy-start(s32[4,1,1024]{2,1,0:T(1,128)} %refs_5_.1) | copy-start | bytes 49156
  0.0 23.0 %copy-start.5 = (s32[4,1,1024]{2,1,0:T(1,128)S(1)}, s32[4,1,1024]{2,1,0:T(1,128)}, u32[]{:S(2)}) copy-start(s32[4,1,1024]{2,1,0:T(1,128)} %refs_6_.1) | copy-start | bytes 49156
  0.0 23.0 %copy-start.6 = (s32[4,1,1024]{2,1,0:T(1,128)S(1)}, s32[4,1,1024]{2,1,0:T(1,128)}, u32[]{:S(2)}) copy-start(s32[4,1,1024]{2,1,0:T(1,128)} %refs_7_.1) | copy-start | bytes 49156
  0.0 23.0 %copy-start.7 = (s32[4096]{0:T(1024)S(1)}, s32[4096]{0:T(1024)}, u32[]{:S(2)}) copy-start(s32[4096]{0:T(1024)} %param.14) | copy-start | bytes 49156
  0.0 23.0 %copy-start.8 = (s32[4096]{0:T(1024)S(1)}, s32[4096]{0:T(1024)}, u32[]{:S(2)}) copy-start(s32[4096]{0:T(1024)} %param.12) | copy-start | bytes 49156
  0.0 23.0 %copy-start.9 = (s32[4096]{0:T(1024)S(1)}, s32[4096]{0:T(1024)}, u32[]{:S(2)}) copy-start(s32[4096]{0:T(1024)} %param.13) | copy-start | bytes 49156
  13.8 13.4 %collective-permute-start.1 = (bf16[120,1024]{1,0:T(8,128)(2,1)S(1)}, bf16[120,1024]{1,0:T(8,128)(2,1)S(1)}, u32[]{:S(2)}, u32[]{:S(2)}) collective-permute-start(bf16[120,1024]{1,0:T(8,128)(2,1)S(1)} %get-tuple-element.25.refs_0_), channel_id=1, source_target_pairs={{4,0},{8,4},{12,8},{16,12},{20,16},{24,20},{28,24},{32,28},{36,32}... | collective-permute-start | bytes 737288 | tf_op jit(solution)/shard_map/ppermute | solution.py:30
  19.8 8.9 %collective-permute-start = (bf16[120,1024]{1,0:T(8,128)(2,1)S(1)}, bf16[120,1024]{1,0:T(8,128)(2,1)S(1)}, u32[]{:S(2)}, u32[]{:S(2)}) collective-permute-start(bf16[120,1024]{1,0:T(8,128)(2,1)S(1)} %get-tuple-element.26.refs_1_), channel_id=1, source_target_pairs={{124,0},{0,4},{4,8},{8,12},{12,16},{16,20},{20,24},{24,28},{28,32}... | collective-permute-start | bytes 737288 | tf_op jit(solution)/shard_map/ppermute | solution.py:30
  19.8 8.9 %collective-permute-start.3 = (bf16[120,1024]{1,0:T(8,128)(2,1)S(1)}, bf16[120,1024]{1,0:T(8,128)(2,1)S(1)}, u32[]{:S(2)}, u32[]{:S(2)}) collective-permute-start(bf16[120,1024]{1,0:T(8,128)(2,1)S(1)} %get-tuple-element.27.refs_2_), channel_id=1, source_target_pairs={{1,0},{2,1},{3,2},{0,3},{5,4},{6,5},{7,6},{4,7},{9,8},{10,9},{11,1... | collective-permute-start | bytes 737288 | tf_op jit(solution)/shard_map/ppermute | solution.py:30
  20.6 8.1 %collective-permute-start.2 = (bf16[120,1024]{1,0:T(8,128)(2,1)S(1)}, bf16[120,1024]{1,0:T(8,128)(2,1)S(1)}, u32[]{:S(2)}, u32[]{:S(2)}) collective-permute-start(bf16[120,1024]{1,0:T(8,128)(2,1)S(1)} %get-tuple-element.28.refs_3_), channel_id=1, source_target_pairs={{3,0},{0,1},{1,2},{2,3},{7,4},{4,5},{5,6},{6,7},{11,8},{8,9},{9,10... | collective-permute-start | bytes 737288 | tf_op jit(solution)/shard_map/ppermute | solution.py:30
  23.1 5.7 %copy-start = (bf16[35,8,4096]{2,1,0:T(8,128)(2,1)S(1)}, bf16[35,8,4096]{2,1,0:T(8,128)(2,1)}, u32[]{:S(2)}) copy-start(bf16[35,8,4096]{2,1,0:T(8,128)(2,1)} %param.11) | copy-start | bytes 6881284
  28.8 34.1 %copy-start.1 = (bf16[6,2,35,35]{3,1,2,0:T(2,128)(2,1)S(1)}, bf16[6,2,35,35]{3,1,2,0:T(2,128)(2,1)}, u32[]{:S(2)}) copy-start(bf16[6,2,35,35]{3,1,2,0:T(2,128)(2,1)} %param.19) | copy-start | bytes 88204
  43.8 8.7 %collective-permute-start.4 = (bf16[288,256]{1,0:T(8,128)(2,1)S(1)}, bf16[288,256]{1,0:T(8,128)(2,1)S(1)}, u32[]{:S(2)}, u32[]{:S(2)}) collective-permute-start(bf16[288,256]{1,0:T(8,128)(2,1)S(1)} %get-tuple-element.35), channel_id=1, source_target_pairs={{127,0},{0,1},{1,2},{2,3},{3,4},{4,5},{5,6},{6,7},{7,8},{8,9},{9,1... | collective-permute-start | bytes 442376 | tf_op jit(solution)/shard_map/ppermute | solution.py:30
  43.9 25.4 %collective-permute-start.5 = (bf16[288,256]{1,0:T(8,128)(2,1)S(1)}, bf16[288,256]{1,0:T(8,128)(2,1)S(1)}, u32[]{:S(2)}, u32[]{:S(2)}) collective-permute-start(bf16[288,256]{1,0:T(8,128)(2,1)S(1)} %get-tuple-element.36), channel_id=1, source_target_pairs={{126,0},{127,1},{0,2},{1,3},{2,4},{3,5},{4,6},{5,7},{6,8},{7,9},{8... | collective-permute-start | bytes 442376 | tf_op jit(solution)/shard_map/ppermute | solution.py:30
  44.0 25.3 %collective-permute-start.6 = (bf16[288,256]{1,0:T(8,128)(2,1)S(1)}, bf16[288,256]{1,0:T(8,128)(2,1)S(1)}, u32[]{:S(2)}, u32[]{:S(2)}) collective-permute-start(bf16[288,256]{1,0:T(8,128)(2,1)S(1)} %get-tuple-element.37), channel_id=1, source_target_pairs={{125,0},{126,1},{127,2},{0,3},{1,4},{2,5},{3,6},{4,7},{5,8},{6,9},... | collective-permute-start | bytes 442376 | tf_op jit(solution)/shard_map/ppermute | solution.py:30
  44.7 24.6 %collective-permute-start.7 = (bf16[288,256]{1,0:T(8,128)(2,1)S(1)}, bf16[288,256]{1,0:T(8,128)(2,1)S(1)}, u32[]{:S(2)}, u32[]{:S(2)}) collective-permute-start(bf16[288,256]{1,0:T(8,128)(2,1)S(1)} %get-tuple-element.38), channel_id=1, source_target_pairs={{1,0},{2,1},{3,2},{4,3},{5,4},{6,5},{7,6},{8,7},{9,8},{10,9},{11,1... | collective-permute-start | bytes 442376 | tf_op jit(solution)/shard_map/ppermute | solution.py:30
  47.0 22.4 %collective-permute-start.8 = (bf16[288,256]{1,0:T(8,128)(2,1)S(1)}, bf16[288,256]{1,0:T(8,128)(2,1)S(1)}, u32[]{:S(2)}, u32[]{:S(2)}) collective-permute-start(bf16[288,256]{1,0:T(8,128)(2,1)S(1)} %get-tuple-element.39), channel_id=1, source_target_pairs={{2,0},{3,1},{4,2},{5,3},{6,4},{7,5},{8,6},{9,7},{10,8},{11,9},{12,... | collective-permute-start | bytes 442376 | tf_op jit(solution)/shard_map/ppermute | solution.py:30
  52.5 16.8 %collective-permute-start.9 = (bf16[288,256]{1,0:T(8,128)(2,1)S(1)}, bf16[288,256]{1,0:T(8,128)(2,1)S(1)}, u32[]{:S(2)}, u32[]{:S(2)}) collective-permute-start(bf16[288,256]{1,0:T(8,128)(2,1)S(1)} %get-tuple-element.40), channel_id=1, source_target_pairs={{3,0},{4,1},{5,2},{6,3},{7,4},{8,5},{9,6},{10,7},{11,8},{12,9},{13... | collective-permute-start | bytes 442376 | tf_op jit(solution)/shard_map/ppermute | solution.py:30

commit v2 on v1

--- a/solution.py
+++ b/solution.py
@@ -20,6 +20,8 @@
 SETS = 4
 LIMIT = 30 << 20
 OFFSETS = (1, 2, 3, -1, -2, -3)
+FORWARD = (1, 2, 0)
+BACKWARD = (4, 5, 3)
 F32 = jnp.float32
 BF16 = jnp.bfloat16
 NT = (((1,), (1,)), ((), ()))
@@ -223,16 +225,15 @@
     )(*owns, *rest)
 
 
-def correct_kernel(tile, *refs):
+def correct_kernel(tile, moves, *refs):
     raised_ref, x_hbm, own_ref = refs[:3]
     near_refs = refs[3:7]
-    meta_ref, table_ref, place_ref, code_ref, fixed_ref = refs[7:12]
-    pack_refs = refs[12:18]
-    lifted_ref, payload_ref, total_ref, x_ref, sems = refs[18:]
+    meta_ref, table_ref, place_ref, code_ref, payload_ref = refs[7:12]
+    pack_refs = refs[12 : 12 + len(moves)]
+    lifted_ref, total_ref, x_ref, sems = refs[12 + len(moves) :]
     copies = fetches((x_hbm,), (x_ref,), sems)
     count = x_ref.shape[1]
     faces = own_ref.shape[2]
-    cap = pack_refs[0].shape[1]
     table = face_table()
 
     def jumps(j, carry):
@@ -262,63 +263,84 @@
     lax.fori_loop(0, faces // tile, jumps, 0)
     copies[0].wait()
 
-    def fix(t, carry):
-        at = pl.ds(pl.multiple_of(t * BUCKET, BUCKET), BUCKET)
-
-        def window(s, i):
-            begin = table_ref[8 * s + t, 0] + i * WINDOW
-            lanes = pl.ds(pl.multiple_of(begin, LANES), WINDOW)
-            return lifted_ref[s, :, lanes], match(BUCKET, meta_ref[s, 0:1, lanes] - t * BUCKET)
-
-        both = [window(s, 0) for s in range(4)]
-        total = x_ref[:, at].astype(F32) + lax.dot_general(
-            jnp.concatenate([a for a, _ in both], axis=1),
-            jnp.concatenate([b for _, b in both], axis=1),
-            NT,
-            preferred_element_type=F32,
-        )
-        total_ref[...] = total
-
-        @pl.when(table_ref[t, 2] > 1)
+    def window(s, t, i):
+        begin = table_ref[8 * s + t, 0] + i * WINDOW
+        lanes = pl.ds(pl.multiple_of(begin, LANES), WINDOW)
+        return lifted_ref[s, :, lanes], match(BUCKET, meta_ref[s, 0:1, lanes] - t * BUCKET)
+
+    def fix(pair, carry):
+        buckets = [2 * pair, 2 * pair + 1]
+        spots = [pl.ds(pl.multiple_of(t * BUCKET, BUCKET), BUCKET) for t in buckets]
+        for u, (t, at) in enumerate(zip(buckets, spots)):
+            both = [window(s, t, 0) for s in range(4)]
+            total_ref[u] = x_ref[:, at].astype(F32) + lax.dot_general(
+                jnp.concatenate([a for a, _ in both], axis=1),
+                jnp.concatenate([b for _, b in both], axis=1),
+                NT,
+                preferred_element_type=F32,
+            )
+
+        @pl.when(jnp.maximum(table_ref[buckets[0], 2], table_ref[buckets[1], 2]) > 1)
         def _():
-            for s in range(4):
-
-                def more(i, carry, s=s):
-                    a, b = window(s, i)
-                    total_ref[...] += lax.dot_general(a, b, NT, preferred_element_type=F32)
-                    return carry
-
-                lax.fori_loop(1, table_ref[8 * s + t, 1], more, 0)
-
-        total = total_ref[...]
-        fixed_ref[:, at] = total.astype(BF16)
-        code = jnp.broadcast_to(code_ref[:, at], (8, BUCKET)).astype(F32)
-        payload_ref[:, at] = jnp.concatenate([total, code], axis=0).astype(BF16)
+            for u, t in enumerate(buckets):
+                for s in range(4):
+
+                    def more(i, carry, s=s, t=t, u=u):
+                        a, b = window(s, t, i)
+                        total_ref[u] += lax.dot_general(a, b, NT, preferred_element_type=F32)
+                        return carry
+
+                    lax.fori_loop(1, table_ref[8 * s + t, 1], more, 0)
+
+        for u, at in enumerate(spots):
+            code = jnp.broadcast_to(code_ref[:, at], (8, BUCKET)).astype(F32)
+            payload_ref[:, at] = jnp.concatenate([total_ref[u], code], axis=0).astype(BF16)
         return carry
 
-    lax.fori_loop(0, count // BUCKET, fix, 0)
-    for k, pack_ref in enumerate(pack_refs):
+    lax.fori_loop(0, count // (2 * BUCKET), fix, 0)
+    pack_moves(moves, payload_ref, place_ref, pack_refs)
+
+
+def pack_moves(moves, payload_ref, place_ref, pack_refs):
+    for k, pack_ref in zip(moves, pack_refs):
+        cap = pack_ref.shape[1]
         packer = match(cap, place_ref[...] - k * cap)
         pack_ref[...] = lax.dot_general(
             payload_ref[...], packer, NT, preferred_element_type=F32
         ).astype(BF16)
 
 
-def correct_call(x, own, near, meta, table, raised, place, code):
+def pack_kernel(moves, payload_ref, place_ref, *pack_refs):
+    pack_moves(moves, payload_ref, place_ref, pack_refs)
+
+
+def pack_call(moves, payload, place):
+    rows, count = payload.shape
+    return pl.pallas_call(
+        functools.partial(pack_kernel, moves),
+        in_specs=[VMEM_SPEC] * 2,
+        out_specs=[VMEM_SPEC] * len(moves),
+        out_shape=[jax.ShapeDtypeStruct((rows, count // 16), BF16)] * len(moves),
+        compiler_params=pltpu.CompilerParams(vmem_limit_bytes=LIMIT),
+        cost_estimate=pl.CostEstimate(flops=2 * 10**9, bytes_accessed=10**6, transcendentals=0),
+        name="pack",
+    )(payload, place)
+
+
+def correct_call(moves, x, own, near, meta, table, raised, place, code):
     count = x.shape[1]
     cap = count // 16
     faces = own.shape[2]
     rows = ROWS + 8
     return pl.pallas_call(
-        functools.partial(correct_kernel, 512),
+        functools.partial(correct_kernel, 512, moves),
         in_specs=[VMEM_SPEC, HBM_SPEC] + [VMEM_SPEC] * 6 + [SMEM_SPEC] + [VMEM_SPEC] * 2,
-        out_specs=[VMEM_SPEC] * 7,
-        out_shape=[jax.ShapeDtypeStruct((ROWS, count), BF16)]
-        + [jax.ShapeDtypeStruct((rows, cap), BF16)] * 6,
+        out_specs=[VMEM_SPEC] * (1 + len(moves)),
+        out_shape=[jax.ShapeDtypeStruct((rows, count), BF16)]
+        + [jax.ShapeDtypeStruct((rows, cap), BF16)] * len(moves),
         scratch_shapes=[
             pltpu.VMEM((4, ROWS, faces + LANES), BF16),
-            pltpu.VMEM((rows, count), BF16),
-            pltpu.VMEM((ROWS, BUCKET), F32),
+            pltpu.VMEM((2, ROWS, BUCKET), F32),
         ]
         + room(x),
         compiler_params=pltpu.CompilerParams(vmem_limit_bytes=LIMIT),
@@ -387,7 +409,7 @@
         def put(child, value, h=h):
             out_ref[child, :, h * PART : (h + 1) * PART] = value
 
-        parents = fixed_ref[:, at].astype(F32)
+        parents = fixed_ref[:ROWS, at].astype(F32)
         bisect_part(weights_ref[...], parents, state_ref[:, at], wide_refs[h], kids_refs[h], put)
 
 
@@ -487,9 +509,12 @@
         refine[None, :],
         edge[None, :],
     )
-    fixed, *packs = correct_call(x, own, near, meta, table, raised, place, code)
-    parts = [passed_along(packs[k], ("gx", "gz"), OFFSETS[k]) for k in range(6)]
-    kept, weights = home_call(fixed, state, prolong, slots)
+    payload, *packs = correct_call(FORWARD, x, own, near, meta, table, raised, place, code)
+    packs += pack_call(BACKWARD, payload, place)
+    parts = [None] * 6
+    for k, pack in zip(FORWARD + BACKWARD, packs):
+        parts[k] = passed_along(pack, ("gx", "gz"), OFFSETS[k])
+    kept, weights = home_call(payload, state, prolong, slots)
     out = incoming_call(parts, weights, kept)
     return out.reshape(2, MODES, FIELDS, slots)
 

time: 72 us -> 66.4 us (0.922)
  starting transfers between devices: 25.8 us -> 22.9 us
  waiting for transfers between devices: 4.01 us -> 1.97 us
  Pallas kernels: 41.7 us -> 40.9 us
    ppermute x10, starting transfers between devices: 25.8 us -> 22.9 us  [passed_along(): lax.ppermute(block, axis, [((i - distance) % count, i) for i in range(cou...]
    ppermute x10, waiting for transfers between devices: 4.01 us -> 1.97 us  [passed_along(): lax.ppermute(block, axis, [((i - distance) % count, i) for i in range(cou...]
    pallas_call x1 -> x2, Pallas kernels: 15 us -> 14.2 us  [the longest x1 12.2 us: correct_call(): pl.pallas_call(functools.partial(correct_kernel, 512, moves), in_specs=[V...]
  transfers between devices with their start and end apart: 10 -> 10, of which waited for: 2 -> 2; matrix products, arithmetic and copies ran while one was open for 0% -> 0% of each run, Pallas kernels for 15% -> 19%
where the time goes in v2:
time: 66.4 us; the launch traced here: 66.2 us
  Pallas kernels  40.9 us (62%)
  starting transfers between devices  22.9 us (34%)
  waiting for transfers between devices  1.97 us (3%)
    ppermute x10, starting transfers between devices, passed_along(): lax.ppermute(block, axis, [((i - distance) % count, i) for i in range(cou...  22.9 us
    pallas_call x1, Pallas kernels, trace_call(): pl.pallas_call(functools.partial(trace_kernel, 1024), in_specs=[HBM_SPEC]...  13.7 us
    pallas_call x1, Pallas kernels, correct_call(): pl.pallas_call(functools.partial(correct_kernel, 512, moves), in_specs=[V...  12.2 us
    pallas_call x1, Pallas kernels, home_call(): pl.pallas_call(home_kernel, grid=(count // tile,), in_specs=[VMEM_SPEC, V...  6.47 us
    pallas_call x1, Pallas kernels, plan_call(): pl.pallas_call(plan_kernel, in_specs=[VMEM_SPEC] * 4 + [HBM_SPEC] * 8, ou...  4.07 us
    pallas_call x1, Pallas kernels, incoming_call(): pl.pallas_call(incoming_kernel, in_specs=[VMEM_SPEC] * 7 + [HBM_SPEC], ou...  2.38 us
    pallas_call x1, Pallas kernels, pack_call(): pl.pallas_call(functools.partial(pack_kernel, moves), in_specs=[VMEM_SPEC...  2.02 us
    ppermute x10, waiting for transfers between devices, passed_along(): lax.ppermute(block, axis, [((i - distance) % count, i) for i in range(cou...  1.97 us
  transfers between devices with their start and end apart: 10, of which 2 were waited for; matrix products, arithmetic and copies ran while one was open for 0% of the time, Pallas kernels for 19%

profile of v2, /device:TPU:6, one launch (start us, length us, event | category | flops | bytes accessed | tf_op | source)
XLA Modules:
  0.0 66.2 jit_solution(3640837920851251455)
XLA Ops:
  0.1 13.7 %trace.1 = (bf16[120,1024]{1,0:T(8,128)(2,1)S(1)}, bf16[120,1024]{1,0:T(8,128)(2,1)S(1)}, bf16[120,1024]{1,0:T(8,128)(2,1)S(1)}, bf16[120,1024]{1,0:T(8,128)(2,1)S(1)}) custom-call(bf16[15,4,35]{2,1,0:T(4,128)(2,1)} %bitcast.15, s32[4,1,1024]{2,1,0:T(1,128)} %refs_4_.1, s32[4,1,1024]{2,1,0:T(1,128)} %refs_5_.1, bf16[280,4096]{1,0:T(8,128)(2,1)} %bitcast.8), custom_call_target="tpu_custom_call" | custom-call | flops 10000000000 | bytes 10000000 | tf_op jit(solution)/shard_map/trace/pallas_call | solution.py:118
  13.8 6.0 %collective-permute-start.1 = (bf16[120,1024]{1,0:T(8,128)(2,1)S(1)}, bf16[120,1024]{1,0:T(8,128)(2,1)S(1)}, u32[]{:S(2)}, u32[]{:S(2)}) collective-permute-start(bf16[120,1024]{1,0:T(8,128)(2,1)S(1)} %get-tuple-element.25.refs_0_), channel_id=1, source_target_pairs={{4,0},{8,4},{12,8},{16,12},{20,16},{24,20},{28,24},{32,28},{36,32}... | collective-permute-start | bytes 737288 | tf_op jit(solution)/shard_map/ppermute | solution.py:32
  19.8 0.0 collective-permute-start
  19.8 0.8 %collective-permute-start.3 = (bf16[120,1024]{1,0:T(8,128)(2,1)S(1)}, bf16[120,1024]{1,0:T(8,128)(2,1)S(1)}, u32[]{:S(2)}, u32[]{:S(2)}) collective-permute-start(bf16[120,1024]{1,0:T(8,128)(2,1)S(1)} %get-tuple-element.27.refs_2_), channel_id=1, source_target_pairs={{1,0},{2,1},{3,2},{0,3},{5,4},{6,5},{7,6},{4,7},{9,8},{10,9},{11,1... | collective-permute-start | bytes 737288 | tf_op jit(solution)/shard_map/ppermute | solution.py:32
  20.6 2.4 %collective-permute-start.2 = (bf16[120,1024]{1,0:T(8,128)(2,1)S(1)}, bf16[120,1024]{1,0:T(8,128)(2,1)S(1)}, u32[]{:S(2)}, u32[]{:S(2)}) collective-permute-start(bf16[120,1024]{1,0:T(8,128)(2,1)S(1)} %get-tuple-element.28.refs_3_), channel_id=1, source_target_pairs={{3,0},{0,1},{1,2},{2,3},{7,4},{4,5},{5,6},{6,7},{11,8},{8,9},{9,10... | collective-permute-start | bytes 737288 | tf_op jit(solution)/shard_map/ppermute | solution.py:32
  23.1 0.0 copy-start
  23.1 4.1 %plan.1 = (bf16[4,120,1024]{2,1,0:T(8,128)(2,1)S(1)}, s32[4,8,1152]{2,1,0:T(8,128)S(1)}, s32[32,128]{1,0:T(8,128)S(1)}, bf16[280,480]{1,0:T(8,128)(2,1)S(1)}, s3...) custom-call(bf16[120,1024]{1,0:T(8,128)(2,1)S(1)} %get-tuple-element.25.refs_0_, ...), custom_call_target="tpu_custom_call" | custom-call | flops 5000000000 | bytes 4000000 | tf_op jit(solution)/shard_map/plan/pallas_call | solution.py:208
  27.2 1.5 %collective-permute-done.refs_3_ = bf16[120,1024]{1,0:T(8,128)(2,1)S(1)} collective-permute-done((bf16[120,1024]{1,0:T(8,128)(2,1)S(1)}, bf16[120,1024]{1,0:T(8,128)(2,1)S(1)}, u32[]{:S(2)}, u32[]{:S(2)}) %collective-permute-start) | collective-permute-done | bytes 245792 | tf_op jit(solution)/shard_map/ppermute | solution.py:32
  28.7 0.0 collective-permute-done.3.refs_6_
  28.8 0.0 collective-permute-done.2.refs_5_
  28.8 12.2 %correct.1 = (bf16[288,4096]{1,0:T(8,128)(2,1)S(1)}, bf16[288,256]{1,0:T(8,128)(2,1)S(1)}, bf16[288,256]{1,0:T(8,128)(2,1)S(1)}, bf16[288,256]{1,0:T(8,128)(2,1)S(1)}) custom-call(bf16[280,480]{1,0:T(8,128)(2,1)S(1)} %get-tuple-element.29.refs_0_, bf16[280,4096]{1,0:T(8,128)(2,1)S(1)} %bitcast.9, bf16[4,120,1024]{2,1,0:T(8,128)(2,1)S(1)} %get-tuple-element.30.refs_2_, ...), custom_call_target="tpu_custom_call" | custom-call | flops 10000000000 | bytes 10000000 | tf_op jit(solution)/shard_map/correct/pallas_call | solution.py:335
  41.0 0.0 copy-start.1
  41.0 0.1 collective-permute-start.4
  41.1 0.1 collective-permute-start.5
  41.2 0.8 %collective-permute-start.6 = (bf16[288,256]{1,0:T(8,128)(2,1)S(1)}, bf16[288,256]{1,0:T(8,128)(2,1)S(1)}, u32[]{:S(2)}, u32[]{:S(2)}) collective-permute-start(bf16[288,256]{1,0:T(8,128)(2,1)S(1)} %get-tuple-element.37), channel_id=1, source_target_pairs={{125,0},{126,1},{127,2},{0,3},{1,4},{2,5},{3,6},{4,7},{5,8},{6,9},... | collective-permute-start | bytes 442376 | tf_op jit(solution)/shard_map/ppermute | solution.py:32
  42.0 2.0 %pack.1 = (bf16[288,256]{1,0:T(8,128)(2,1)S(1)}, bf16[288,256]{1,0:T(8,128)(2,1)S(1)}, bf16[288,256]{1,0:T(8,128)(2,1)S(1)}) custom-call(bf16[288,4096]{1,0:T(8,128)(2,1)S(1)} %get-tuple-element.38.payload_ref.fixed_ref, s32[1,4096]{1,0:T(1,128)S(1)} %get-tuple-element.33.refs_9_.place_ref), custom_call_target="tpu_custom_call" | custom-call | flops 2000000000 | bytes 1000000 | tf_op jit(solution)/shard_map/pack/pallas_call | solution.py:319
  44.0 2.3 %collective-permute-start.7 = (bf16[288,256]{1,0:T(8,128)(2,1)S(1)}, bf16[288,256]{1,0:T(8,128)(2,1)S(1)}, u32[]{:S(2)}, u32[]{:S(2)}) collective-permute-start(bf16[288,256]{1,0:T(8,128)(2,1)S(1)} %get-tuple-element.39), channel_id=1, source_target_pairs={{1,0},{2,1},{3,2},{4,3},{5,4},{6,5},{7,6},{8,7},{9,8},{10,9},{11,1... | collective-permute-start | bytes 442376 | tf_op jit(solution)/shard_map/ppermute | solution.py:32
  46.3 3.0 %collective-permute-start.8 = (bf16[288,256]{1,0:T(8,128)(2,1)S(1)}, bf16[288,256]{1,0:T(8,128)(2,1)S(1)}, u32[]{:S(2)}, u32[]{:S(2)}) collective-permute-start(bf16[288,256]{1,0:T(8,128)(2,1)S(1)} %get-tuple-element.40), channel_id=1, source_target_pairs={{2,0},{3,1},{4,2},{5,3},{6,4},{7,5},{8,6},{9,7},{10,8},{11,9},{12,... | collective-permute-start | bytes 442376 | tf_op jit(solution)/shard_map/ppermute | solution.py:32
  49.3 0.4 collective-permute-done.4.refs_0_
  49.8 7.4 %collective-permute-start.9 = (bf16[288,256]{1,0:T(8,128)(2,1)S(1)}, bf16[288,256]{1,0:T(8,128)(2,1)S(1)}, u32[]{:S(2)}, u32[]{:S(2)}) collective-permute-start(bf16[288,256]{1,0:T(8,128)(2,1)S(1)} %get-tuple-element.41), channel_id=1, source_target_pairs={{3,0},{4,1},{5,2},{6,3},{7,4},{8,5},{9,6},{10,7},{11,8},{12,9},{13... | collective-permute-start | bytes 442376 | tf_op jit(solution)/shard_map/ppermute | solution.py:32
  57.2 6.5 %home.1 = (bf16[2,280,5632]{2,1,0:T(8,128)(2,1)}, bf16[80,240]{1,0:T(8,128)(2,1)S(1)}) custom-call(bf16[288,4096]{1,0:T(8,128)(2,1)S(1)} %get-tuple-element.38.payload_ref.fixed_ref, s32[1,4096]{1,0:T(1,128)S(1)} %get-tuple-element.42.state_ref, bf16[6,35,2,35]{3,2,1,0:T(2,128)(2,1)S(1)} %bitcast.10), custom_call_target="tpu_custom_call" | custom-call | flops 1284505600 | bytes 6881280 | tf_op jit(solution)/shard_map/home/pallas_call | solution.py:419
  63.6 0.0 collective-permute-done.7.refs_3_
  63.7 0.0 collective-permute-done.9.refs_5_
  63.7 2.4 %incoming.1 = bf16[2,280,5632]{2,1,0:T(8,128)(2,1)} custom-call(bf16[288,256]{1,0:T(8,128)(2,1)S(1)} %collective-permute-done.4.refs_0_, bf16[288,256]{1,0:T(8,128)(2,1)S(1)} %collective-permute-done.5.refs_1_, bf16[288,256]{1,0:T(8,128)(2,1)S(1)} %collective-permute-done.6.refs_2_, ...), custom_call_target="tpu_custom_call", output_to_operand_aliasing={{}: (7, {})} | custom-call | tf_op jit(solution)/shard_map/incoming/pallas_call | solution.py:465
  (22 shorter events, 0.0 us)
Async XLA Ops:
  0.0 23.0 %copy-start.2 = (f32[4,35,15]{1,0,2:T(4,128)S(1)}, f32[4,35,15]{1,0,2:T(4,128)}, u32[]{:S(2)}) copy-start(f32[4,35,15]{1,0,2:T(4,128)} %param.21) | copy-start | bytes 25204
  0.0 23.0 %copy-start.3 = (s32[4,1,1024]{2,1,0:T(1,128)S(1)}, s32[4,1,1024]{2,1,0:T(1,128)}, u32[]{:S(2)}) copy-start(s32[4,1,1024]{2,1,0:T(1,128)} %refs_4_.1) | copy-start | bytes 49156
  0.0 23.0 %copy-start.4 = (s32[4,1,1024]{2,1,0:T(1,128)S(1)}, s32[4,1,1024]{2,1,0:T(1,128)}, u32[]{:S(2)}) copy-start(s32[4,1,1024]{2,1,0:T(1,128)} %refs_5_.1) | copy-start | bytes 49156
  0.0 23.0 %copy-start.5 = (s32[4,1,1024]{2,1,0:T(1,128)S(1)}, s32[4,1,1024]{2,1,0:T(1,128)}, u32[]{:S(2)}) copy-start(s32[4,1,1024]{2,1,0:T(1,128)} %refs_6_.1) | copy-start | bytes 49156
  0.0 23.0 %copy-start.6 = (s32[4,1,1024]{2,1,0:T(1,128)S(1)}, s32[4,1,1024]{2,1,0:T(1,128)}, u32[]{:S(2)}) copy-start(s32[4,1,1024]{2,1,0:T(1,128)} %refs_7_.1) | copy-start | bytes 49156
  0.0 23.0 %copy-start.7 = (s32[4096]{0:T(1024)S(1)}, s32[4096]{0:T(1024)}, u32[]{:S(2)}) copy-start(s32[4096]{0:T(1024)} %param.14) | copy-start | bytes 49156
  0.0 23.0 %copy-start.8 = (s32[4096]{0:T(1024)S(1)}, s32[4096]{0:T(1024)}, u32[]{:S(2)}) copy-start(s32[4096]{0:T(1024)} %param.12) | copy-start | bytes 49156
  0.0 23.0 %copy-start.9 = (s32[4096]{0:T(1024)S(1)}, s32[4096]{0:T(1024)}, u32[]{:S(2)}) copy-start(s32[4096]{0:T(1024)} %param.13) | copy-start | bytes 49156
  13.8 13.4 %collective-permute-start.1 = (bf16[120,1024]{1,0:T(8,128)(2,1)S(1)}, bf16[120,1024]{1,0:T(8,128)(2,1)S(1)}, u32[]{:S(2)}, u32[]{:S(2)}) collective-permute-start(bf16[120,1024]{1,0:T(8,128)(2,1)S(1)} %get-tuple-element.25.refs_0_), channel_id=1, source_target_pairs={{4,0},{8,4},{12,8},{16,12},{20,16},{24,20},{28,24},{32,28},{36,32}... | collective-permute-start | bytes 737288 | tf_op jit(solution)/shard_map/ppermute | solution.py:32
  19.8 8.9 %collective-permute-start = (bf16[120,1024]{1,0:T(8,128)(2,1)S(1)}, bf16[120,1024]{1,0:T(8,128)(2,1)S(1)}, u32[]{:S(2)}, u32[]{:S(2)}) collective-permute-start(bf16[120,1024]{1,0:T(8,128)(2,1)S(1)} %get-tuple-element.26.refs_1_), channel_id=1, source_target_pairs={{124,0},{0,4},{4,8},{8,12},{12,16},{16,20},{20,24},{24,28},{28,32}... | collective-permute-start | bytes 737288 | tf_op jit(solution)/shard_map/ppermute | solution.py:32
  19.8 8.9 %collective-permute-start.3 = (bf16[120,1024]{1,0:T(8,128)(2,1)S(1)}, bf16[120,1024]{1,0:T(8,128)(2,1)S(1)}, u32[]{:S(2)}, u32[]{:S(2)}) collective-permute-start(bf16[120,1024]{1,0:T(8,128)(2,1)S(1)} %get-tuple-element.27.refs_2_), channel_id=1, source_target_pairs={{1,0},{2,1},{3,2},{0,3},{5,4},{6,5},{7,6},{4,7},{9,8},{10,9},{11,1... | collective-permute-start | bytes 737288 | tf_op jit(solution)/shard_map/ppermute | solution.py:32
  20.6 8.1 %collective-permute-start.2 = (bf16[120,1024]{1,0:T(8,128)(2,1)S(1)}, bf16[120,1024]{1,0:T(8,128)(2,1)S(1)}, u32[]{:S(2)}, u32[]{:S(2)}) collective-permute-start(bf16[120,1024]{1,0:T(8,128)(2,1)S(1)} %get-tuple-element.28.refs_3_), channel_id=1, source_target_pairs={{3,0},{0,1},{1,2},{2,3},{7,4},{4,5},{5,6},{6,7},{11,8},{8,9},{9,10... | collective-permute-start | bytes 737288 | tf_op jit(solution)/shard_map/ppermute | solution.py:32
  23.1 5.7 %copy-start = (bf16[35,8,4096]{2,1,0:T(8,128)(2,1)S(1)}, bf16[35,8,4096]{2,1,0:T(8,128)(2,1)}, u32[]{:S(2)}) copy-start(bf16[35,8,4096]{2,1,0:T(8,128)(2,1)} %param.11) | copy-start | bytes 6881284
  41.0 16.2 %copy-start.1 = (bf16[6,2,35,35]{3,1,2,0:T(2,128)(2,1)S(1)}, bf16[6,2,35,35]{3,1,2,0:T(2,128)(2,1)}, u32[]{:S(2)}) copy-start(bf16[6,2,35,35]{3,1,2,0:T(2,128)(2,1)} %param.19) | copy-start | bytes 88204
  41.0 8.8 %collective-permute-start.4 = (bf16[288,256]{1,0:T(8,128)(2,1)S(1)}, bf16[288,256]{1,0:T(8,128)(2,1)S(1)}, u32[]{:S(2)}, u32[]{:S(2)}) collective-permute-start(bf16[288,256]{1,0:T(8,128)(2,1)S(1)} %get-tuple-element.35), channel_id=1, source_target_pairs={{127,0},{0,1},{1,2},{2,3},{3,4},{4,5},{5,6},{6,7},{7,8},{8,9},{9,1... | collective-permute-start | bytes 442376 | tf_op jit(solution)/shard_map/ppermute | solution.py:32
  41.1 22.6 %collective-permute-start.5 = (bf16[288,256]{1,0:T(8,128)(2,1)S(1)}, bf16[288,256]{1,0:T(8,128)(2,1)S(1)}, u32[]{:S(2)}, u32[]{:S(2)}) collective-permute-start(bf16[288,256]{1,0:T(8,128)(2,1)S(1)} %get-tuple-element.36), channel_id=1, source_target_pairs={{126,0},{127,1},{0,2},{1,3},{2,4},{3,5},{4,6},{5,7},{6,8},{7,9},{8... | collective-permute-start | bytes 442376 | tf_op jit(solution)/shard_map/ppermute | solution.py:32
  41.2 22.5 %collective-permute-start.6 = (bf16[288,256]{1,0:T(8,128)(2,1)S(1)}, bf16[288,256]{1,0:T(8,128)(2,1)S(1)}, u32[]{:S(2)}, u32[]{:S(2)}) collective-permute-start(bf16[288,256]{1,0:T(8,128)(2,1)S(1)} %get-tuple-element.37), channel_id=1, source_target_pairs={{125,0},{126,1},{127,2},{0,3},{1,4},{2,5},{3,6},{4,7},{5,8},{6,9},... | collective-permute-start | bytes 442376 | tf_op jit(solution)/shard_map/ppermute | solution.py:32
  44.0 19.6 %collective-permute-start.7 = (bf16[288,256]{1,0:T(8,128)(2,1)S(1)}, bf16[288,256]{1,0:T(8,128)(2,1)S(1)}, u32[]{:S(2)}, u32[]{:S(2)}) collective-permute-start(bf16[288,256]{1,0:T(8,128)(2,1)S(1)} %get-tuple-element.39), channel_id=1, source_target_pairs={{1,0},{2,1},{3,2},{4,3},{5,4},{6,5},{7,6},{8,7},{9,8},{10,9},{11,1... | collective-permute-start | bytes 442376 | tf_op jit(solution)/shard_map/ppermute | solution.py:32
  46.3 17.3 %collective-permute-start.8 = (bf16[288,256]{1,0:T(8,128)(2,1)S(1)}, bf16[288,256]{1,0:T(8,128)(2,1)S(1)}, u32[]{:S(2)}, u32[]{:S(2)}) collective-permute-start(bf16[288,256]{1,0:T(8,128)(2,1)S(1)} %get-tuple-element.40), channel_id=1, source_target_pairs={{2,0},{3,1},{4,2},{5,3},{6,4},{7,5},{8,6},{9,7},{10,8},{11,9},{12,... | collective-permute-start | bytes 442376 | tf_op jit(solution)/shard_map/ppermute | solution.py:32
  49.8 13.9 %collective-permute-start.9 = (bf16[288,256]{1,0:T(8,128)(2,1)S(1)}, bf16[288,256]{1,0:T(8,128)(2,1)S(1)}, u32[]{:S(2)}, u32[]{:S(2)}) collective-permute-start(bf16[288,256]{1,0:T(8,128)(2,1)S(1)} %get-tuple-element.41), channel_id=1, source_target_pairs={{3,0},{4,1},{5,2},{6,3},{7,4},{8,5},{9,6},{10,7},{11,8},{12,9},{13... | collective-permute-start | bytes 442376 | tf_op jit(solution)/shard_map/ppermute | solution.py:32

commit v3 on v2

--- a/solution.py
+++ b/solution.py
@@ -302,12 +302,12 @@
 
 
 def pack_moves(moves, payload_ref, place_ref, pack_refs):
+    cap = pack_refs[0].shape[1]
+    low = min(moves)
+    packer = match(len(moves) * cap, place_ref[...] - low * cap)
+    packed = lax.dot_general(payload_ref[...], packer, NT, preferred_element_type=F32)
     for k, pack_ref in zip(moves, pack_refs):
-        cap = pack_ref.shape[1]
-        packer = match(cap, place_ref[...] - k * cap)
-        pack_ref[...] = lax.dot_general(
-            payload_ref[...], packer, NT, preferred_element_type=F32
-        ).astype(BF16)
+        pack_ref[...] = packed[:, (k - low) * cap : (k - low + 1) * cap].astype(BF16)
 
 
 def pack_kernel(moves, payload_ref, place_ref, *pack_refs):
@@ -333,7 +333,7 @@
     faces = own.shape[2]
     rows = ROWS + 8
     return pl.pallas_call(
-        functools.partial(correct_kernel, 512, moves),
+        functools.partial(correct_kernel, 1024, moves),
         in_specs=[VMEM_SPEC, HBM_SPEC] + [VMEM_SPEC] * 6 + [SMEM_SPEC] + [VMEM_SPEC] * 2,
         out_specs=[VMEM_SPEC] * (1 + len(moves)),
         out_shape=[jax.ShapeDtypeStruct((rows, count), BF16)]

time: 66.4 us -> 64.9 us (0.977)
  Pallas kernels: 40.9 us -> 39.4 us
    pallas_call x1, Pallas kernels: 12.2 us -> 10.8 us  [correct_call(): pl.pallas_call(functools.partial(correct_kernel, 1024, moves), in_specs=[...]
where the time goes in v3:
time: 64.9 us; the launch traced here: 64.8 us
  Pallas kernels  39.4 us (61%)
  starting transfers between devices  22.9 us (35%)
  waiting for transfers between devices  1.97 us (3%)
    ppermute x10, starting transfers between devices, passed_along(): lax.ppermute(block, axis, [((i - distance) % count, i) for i in range(cou...  22.9 us
    pallas_call x1, Pallas kernels, trace_call(): pl.pallas_call(functools.partial(trace_kernel, 1024), in_specs=[HBM_SPEC]...  13.7 us
    pallas_call x1, Pallas kernels, correct_call(): pl.pallas_call(functools.partial(correct_kernel, 1024, moves), in_specs=[...  10.8 us
    pallas_call x1, Pallas kernels, home_call(): pl.pallas_call(home_kernel, grid=(count // tile,), in_specs=[VMEM_SPEC, V...  6.47 us
    pallas_call x1, Pallas kernels, plan_call(): pl.pallas_call(plan_kernel, in_specs=[VMEM_SPEC] * 4 + [HBM_SPEC] * 8, ou...  4.07 us
    pallas_call x1, Pallas kernels, incoming_call(): pl.pallas_call(incoming_kernel, in_specs=[VMEM_SPEC] * 7 + [HBM_SPEC], ou...  2.38 us
    pallas_call x1, Pallas kernels, pack_call(): pl.pallas_call(functools.partial(pack_kernel, moves), in_specs=[VMEM_SPEC...  2.02 us
    ppermute x10, waiting for transfers between devices, passed_along(): lax.ppermute(block, axis, [((i - distance) % count, i) for i in range(cou...  1.97 us
  transfers between devices with their start and end apart: 10, of which 2 were waited for; matrix products, arithmetic and copies ran while one was open for 0% of the time, Pallas kernels for 19%

profile of v3, /device:TPU:6, one launch (start us, length us, event | category | flops | bytes accessed | tf_op | source)
XLA Modules:
  0.0 64.8 jit_solution(15150026478268350148)
XLA Ops:
  0.1 13.7 %trace.1 = (bf16[120,1024]{1,0:T(8,128)(2,1)S(1)}, bf16[120,1024]{1,0:T(8,128)(2,1)S(1)}, bf16[120,1024]{1,0:T(8,128)(2,1)S(1)}, bf16[120,1024]{1,0:T(8,128)(2,1)S(1)}) custom-call(bf16[15,4,35]{2,1,0:T(4,128)(2,1)} %bitcast.15, s32[4,1,1024]{2,1,0:T(1,128)} %refs_4_.1, s32[4,1,1024]{2,1,0:T(1,128)} %refs_5_.1, bf16[280,4096]{1,0:T(8,128)(2,1)} %bitcast.8), custom_call_target="tpu_custom_call" | custom-call | flops 10000000000 | bytes 10000000 | tf_op jit(solution)/shard_map/trace/pallas_call | solution.py:118
  13.8 6.0 %collective-permute-start.1 = (bf16[120,1024]{1,0:T(8,128)(2,1)S(1)}, bf16[120,1024]{1,0:T(8,128)(2,1)S(1)}, u32[]{:S(2)}, u32[]{:S(2)}) collective-permute-start(bf16[120,1024]{1,0:T(8,128)(2,1)S(1)} %get-tuple-element.25.refs_0_), channel_id=1, source_target_pairs={{4,0},{8,4},{12,8},{16,12},{20,16},{24,20},{28,24},{32,28},{36,32}... | collective-permute-start | bytes 737288 | tf_op jit(solution)/shard_map/ppermute | solution.py:32
  19.8 0.8 %collective-permute-start.3 = (bf16[120,1024]{1,0:T(8,128)(2,1)S(1)}, bf16[120,1024]{1,0:T(8,128)(2,1)S(1)}, u32[]{:S(2)}, u32[]{:S(2)}) collective-permute-start(bf16[120,1024]{1,0:T(8,128)(2,1)S(1)} %get-tuple-element.27.refs_2_), channel_id=1, source_target_pairs={{1,0},{2,1},{3,2},{0,3},{5,4},{6,5},{7,6},{4,7},{9,8},{10,9},{11,1... | collective-permute-start | bytes 737288 | tf_op jit(solution)/shard_map/ppermute | solution.py:32
  20.6 2.4 %collective-permute-start.2 = (bf16[120,1024]{1,0:T(8,128)(2,1)S(1)}, bf16[120,1024]{1,0:T(8,128)(2,1)S(1)}, u32[]{:S(2)}, u32[]{:S(2)}) collective-permute-start(bf16[120,1024]{1,0:T(8,128)(2,1)S(1)} %get-tuple-element.28.refs_3_), channel_id=1, source_target_pairs={{3,0},{0,1},{1,2},{2,3},{7,4},{4,5},{5,6},{6,7},{11,8},{8,9},{9,10... | collective-permute-start | bytes 737288 | tf_op jit(solution)/shard_map/ppermute | solution.py:32
  23.1 0.0 copy-start
  23.1 4.1 %plan.1 = (bf16[4,120,1024]{2,1,0:T(8,128)(2,1)S(1)}, s32[4,8,1152]{2,1,0:T(8,128)S(1)}, s32[32,128]{1,0:T(8,128)S(1)}, bf16[280,480]{1,0:T(8,128)(2,1)S(1)}, s3...) custom-call(bf16[120,1024]{1,0:T(8,128)(2,1)S(1)} %get-tuple-element.25.refs_0_, ...), custom_call_target="tpu_custom_call" | custom-call | flops 5000000000 | bytes 4000000 | tf_op jit(solution)/shard_map/plan/pallas_call | solution.py:208
  27.2 1.5 %collective-permute-done.refs_3_ = bf16[120,1024]{1,0:T(8,128)(2,1)S(1)} collective-permute-done((bf16[120,1024]{1,0:T(8,128)(2,1)S(1)}, bf16[120,1024]{1,0:T(8,128)(2,1)S(1)}, u32[]{:S(2)}, u32[]{:S(2)}) %collective-permute-start) | collective-permute-done | bytes 245792 | tf_op jit(solution)/shard_map/ppermute | solution.py:32
  28.7 0.0 collective-permute-done.3.refs_6_
  28.8 0.0 collective-permute-done.2.refs_5_
  28.8 10.8 %correct.1 = (bf16[288,4096]{1,0:T(8,128)(2,1)S(1)}, bf16[288,256]{1,0:T(8,128)(2,1)S(1)}, bf16[288,256]{1,0:T(8,128)(2,1)S(1)}, bf16[288,256]{1,0:T(8,128)(2,1)S(1)}) custom-call(bf16[280,480]{1,0:T(8,128)(2,1)S(1)} %get-tuple-element.29.refs_0_, bf16[280,4096]{1,0:T(8,128)(2,1)S(1)} %bitcast.9, bf16[4,120,1024]{2,1,0:T(8,128)(2,1)S(1)} %get-tuple-element.30.refs_2_, ...), custom_call_target="tpu_custom_call" | custom-call | flops 10000000000 | bytes 10000000 | tf_op jit(solution)/shard_map/correct/pallas_call | solution.py:335
  39.5 0.0 copy-start.1
  39.5 0.1 collective-permute-start.4
  39.6 0.1 collective-permute-start.5
  39.7 0.8 %collective-permute-start.6 = (bf16[288,256]{1,0:T(8,128)(2,1)S(1)}, bf16[288,256]{1,0:T(8,128)(2,1)S(1)}, u32[]{:S(2)}, u32[]{:S(2)}) collective-permute-start(bf16[288,256]{1,0:T(8,128)(2,1)S(1)} %get-tuple-element.37), channel_id=1, source_target_pairs={{125,0},{126,1},{127,2},{0,3},{1,4},{2,5},{3,6},{4,7},{5,8},{6,9},... | collective-permute-start | bytes 442376 | tf_op jit(solution)/shard_map/ppermute | solution.py:32
  40.5 2.0 %pack.1 = (bf16[288,256]{1,0:T(8,128)(2,1)S(1)}, bf16[288,256]{1,0:T(8,128)(2,1)S(1)}, bf16[288,256]{1,0:T(8,128)(2,1)S(1)}) custom-call(bf16[288,4096]{1,0:T(8,128)(2,1)S(1)} %get-tuple-element.38.payload_ref.fixed_ref, s32[1,4096]{1,0:T(1,128)S(1)} %get-tuple-element.33.refs_9_.place_ref), custom_call_target="tpu_custom_call" | custom-call | flops 2000000000 | bytes 1000000 | tf_op jit(solution)/shard_map/pack/pallas_call | solution.py:319
  42.5 2.3 %collective-permute-start.7 = (bf16[288,256]{1,0:T(8,128)(2,1)S(1)}, bf16[288,256]{1,0:T(8,128)(2,1)S(1)}, u32[]{:S(2)}, u32[]{:S(2)}) collective-permute-start(bf16[288,256]{1,0:T(8,128)(2,1)S(1)} %get-tuple-element.39), channel_id=1, source_target_pairs={{1,0},{2,1},{3,2},{4,3},{5,4},{6,5},{7,6},{8,7},{9,8},{10,9},{11,1... | collective-permute-start | bytes 442376 | tf_op jit(solution)/shard_map/ppermute | solution.py:32
  44.9 3.0 %collective-permute-start.8 = (bf16[288,256]{1,0:T(8,128)(2,1)S(1)}, bf16[288,256]{1,0:T(8,128)(2,1)S(1)}, u32[]{:S(2)}, u32[]{:S(2)}) collective-permute-start(bf16[288,256]{1,0:T(8,128)(2,1)S(1)} %get-tuple-element.40), channel_id=1, source_target_pairs={{2,0},{3,1},{4,2},{5,3},{6,4},{7,5},{8,6},{9,7},{10,8},{11,9},{12,... | collective-permute-start | bytes 442376 | tf_op jit(solution)/shard_map/ppermute | solution.py:32
  47.9 0.4 collective-permute-done.4.refs_0_
  48.3 7.4 %collective-permute-start.9 = (bf16[288,256]{1,0:T(8,128)(2,1)S(1)}, bf16[288,256]{1,0:T(8,128)(2,1)S(1)}, u32[]{:S(2)}, u32[]{:S(2)}) collective-permute-start(bf16[288,256]{1,0:T(8,128)(2,1)S(1)} %get-tuple-element.41), channel_id=1, source_target_pairs={{3,0},{4,1},{5,2},{6,3},{7,4},{8,5},{9,6},{10,7},{11,8},{12,9},{13... | collective-permute-start | bytes 442376 | tf_op jit(solution)/shard_map/ppermute | solution.py:32
  55.7 6.5 %home.1 = (bf16[2,280,5632]{2,1,0:T(8,128)(2,1)}, bf16[80,240]{1,0:T(8,128)(2,1)S(1)}) custom-call(bf16[288,4096]{1,0:T(8,128)(2,1)S(1)} %get-tuple-element.38.payload_ref.fixed_ref, s32[1,4096]{1,0:T(1,128)S(1)} %get-tuple-element.42.state_ref, bf16[6,35,2,35]{3,2,1,0:T(2,128)(2,1)S(1)} %bitcast.10), custom_call_target="tpu_custom_call" | custom-call | flops 1284505600 | bytes 6881280 | tf_op jit(solution)/shard_map/home/pallas_call | solution.py:419
  62.2 0.0 collective-permute-done.5.refs_1_
  62.2 0.0 collective-permute-done.6.refs_2_
  62.2 0.0 collective-permute-done.7.refs_3_
  62.2 2.4 %incoming.1 = bf16[2,280,5632]{2,1,0:T(8,128)(2,1)} custom-call(bf16[288,256]{1,0:T(8,128)(2,1)S(1)} %collective-permute-done.4.refs_0_, bf16[288,256]{1,0:T(8,128)(2,1)S(1)} %collective-permute-done.5.refs_1_, bf16[288,256]{1,0:T(8,128)(2,1)S(1)} %collective-permute-done.6.refs_2_, ...), custom_call_target="tpu_custom_call", output_to_operand_aliasing={{}: (7, {})} | custom-call | tf_op jit(solution)/shard_map/incoming/pallas_call | solution.py:465
  (22 shorter events, 0.0 us)
Async XLA Ops:
  0.0 23.0 %copy-start.2 = (f32[4,35,15]{1,0,2:T(4,128)S(1)}, f32[4,35,15]{1,0,2:T(4,128)}, u32[]{:S(2)}) copy-start(f32[4,35,15]{1,0,2:T(4,128)} %param.21) | copy-start | bytes 25204
  0.0 23.0 %copy-start.3 = (s32[4,1,1024]{2,1,0:T(1,128)S(1)}, s32[4,1,1024]{2,1,0:T(1,128)}, u32[]{:S(2)}) copy-start(s32[4,1,1024]{2,1,0:T(1,128)} %refs_4_.1) | copy-start | bytes 49156
  0.0 23.0 %copy-start.4 = (s32[4,1,1024]{2,1,0:T(1,128)S(1)}, s32[4,1,1024]{2,1,0:T(1,128)}, u32[]{:S(2)}) copy-start(s32[4,1,1024]{2,1,0:T(1,128)} %refs_5_.1) | copy-start | bytes 49156
  0.0 23.0 %copy-start.5 = (s32[4,1,1024]{2,1,0:T(1,128)S(1)}, s32[4,1,1024]{2,1,0:T(1,128)}, u32[]{:S(2)}) copy-start(s32[4,1,1024]{2,1,0:T(1,128)} %refs_6_.1) | copy-start | bytes 49156
  0.0 23.0 %copy-start.6 = (s32[4,1,1024]{2,1,0:T(1,128)S(1)}, s32[4,1,1024]{2,1,0:T(1,128)}, u32[]{:S(2)}) copy-start(s32[4,1,1024]{2,1,0:T(1,128)} %refs_7_.1) | copy-start | bytes 49156
  0.0 23.0 %copy-start.7 = (s32[4096]{0:T(1024)S(1)}, s32[4096]{0:T(1024)}, u32[]{:S(2)}) copy-start(s32[4096]{0:T(1024)} %param.14) | copy-start | bytes 49156
  0.0 23.0 %copy-start.8 = (s32[4096]{0:T(1024)S(1)}, s32[4096]{0:T(1024)}, u32[]{:S(2)}) copy-start(s32[4096]{0:T(1024)} %param.12) | copy-start | bytes 49156
  0.0 23.0 %copy-start.9 = (s32[4096]{0:T(1024)S(1)}, s32[4096]{0:T(1024)}, u32[]{:S(2)}) copy-start(s32[4096]{0:T(1024)} %param.13) | copy-start | bytes 49156
  13.8 13.4 %collective-permute-start.1 = (bf16[120,1024]{1,0:T(8,128)(2,1)S(1)}, bf16[120,1024]{1,0:T(8,128)(2,1)S(1)}, u32[]{:S(2)}, u32[]{:S(2)}) collective-permute-start(bf16[120,1024]{1,0:T(8,128)(2,1)S(1)} %get-tuple-element.25.refs_0_), channel_id=1, source_target_pairs={{4,0},{8,4},{12,8},{16,12},{20,16},{24,20},{28,24},{32,28},{36,32}... | collective-permute-start | bytes 737288 | tf_op jit(solution)/shard_map/ppermute | solution.py:32
  19.8 8.9 %collective-permute-start = (bf16[120,1024]{1,0:T(8,128)(2,1)S(1)}, bf16[120,1024]{1,0:T(8,128)(2,1)S(1)}, u32[]{:S(2)}, u32[]{:S(2)}) collective-permute-start(bf16[120,1024]{1,0:T(8,128)(2,1)S(1)} %get-tuple-element.26.refs_1_), channel_id=1, source_target_pairs={{124,0},{0,4},{4,8},{8,12},{12,16},{16,20},{20,24},{24,28},{28,32}... | collective-permute-start | bytes 737288 | tf_op jit(solution)/shard_map/ppermute | solution.py:32
  19.8 8.9 %collective-permute-start.3 = (bf16[120,1024]{1,0:T(8,128)(2,1)S(1)}, bf16[120,1024]{1,0:T(8,128)(2,1)S(1)}, u32[]{:S(2)}, u32[]{:S(2)}) collective-permute-start(bf16[120,1024]{1,0:T(8,128)(2,1)S(1)} %get-tuple-element.27.refs_2_), channel_id=1, source_target_pairs={{1,0},{2,1},{3,2},{0,3},{5,4},{6,5},{7,6},{4,7},{9,8},{10,9},{11,1... | collective-permute-start | bytes 737288 | tf_op jit(solution)/shard_map/ppermute | solution.py:32
  20.6 8.1 %collective-permute-start.2 = (bf16[120,1024]{1,0:T(8,128)(2,1)S(1)}, bf16[120,1024]{1,0:T(8,128)(2,1)S(1)}, u32[]{:S(2)}, u32[]{:S(2)}) collective-permute-start(bf16[120,1024]{1,0:T(8,128)(2,1)S(1)} %get-tuple-element.28.refs_3_), channel_id=1, source_target_pairs={{3,0},{0,1},{1,2},{2,3},{7,4},{4,5},{5,6},{6,7},{11,8},{8,9},{9,10... | collective-permute-start | bytes 737288 | tf_op jit(solution)/shard_map/ppermute | solution.py:32
  23.1 5.7 %copy-start = (bf16[35,8,4096]{2,1,0:T(8,128)(2,1)S(1)}, bf16[35,8,4096]{2,1,0:T(8,128)(2,1)}, u32[]{:S(2)}) copy-start(bf16[35,8,4096]{2,1,0:T(8,128)(2,1)} %param.11) | copy-start | bytes 6881284
  39.5 16.2 %copy-start.1 = (bf16[6,2,35,35]{3,1,2,0:T(2,128)(2,1)S(1)}, bf16[6,2,35,35]{3,1,2,0:T(2,128)(2,1)}, u32[]{:S(2)}) copy-start(bf16[6,2,35,35]{3,1,2,0:T(2,128)(2,1)} %param.19) | copy-start | bytes 88204
  39.5 8.8 %collective-permute-start.4 = (bf16[288,256]{1,0:T(8,128)(2,1)S(1)}, bf16[288,256]{1,0:T(8,128)(2,1)S(1)}, u32[]{:S(2)}, u32[]{:S(2)}) collective-permute-start(bf16[288,256]{1,0:T(8,128)(2,1)S(1)} %get-tuple-element.35), channel_id=1, source_target_pairs={{127,0},{0,1},{1,2},{2,3},{3,4},{4,5},{5,6},{6,7},{7,8},{8,9},{9,1... | collective-permute-start | bytes 442376 | tf_op jit(solution)/shard_map/ppermute | solution.py:32
  39.6 22.6 %collective-permute-start.5 = (bf16[288,256]{1,0:T(8,128)(2,1)S(1)}, bf16[288,256]{1,0:T(8,128)(2,1)S(1)}, u32[]{:S(2)}, u32[]{:S(2)}) collective-permute-start(bf16[288,256]{1,0:T(8,128)(2,1)S(1)} %get-tuple-element.36), channel_id=1, source_target_pairs={{126,0},{127,1},{0,2},{1,3},{2,4},{3,5},{4,6},{5,7},{6,8},{7,9},{8... | collective-permute-start | bytes 442376 | tf_op jit(solution)/shard_map/ppermute | solution.py:32
  39.7 22.5 %collective-permute-start.6 = (bf16[288,256]{1,0:T(8,128)(2,1)S(1)}, bf16[288,256]{1,0:T(8,128)(2,1)S(1)}, u32[]{:S(2)}, u32[]{:S(2)}) collective-permute-start(bf16[288,256]{1,0:T(8,128)(2,1)S(1)} %get-tuple-element.37), channel_id=1, source_target_pairs={{125,0},{126,1},{127,2},{0,3},{1,4},{2,5},{3,6},{4,7},{5,8},{6,9},... | collective-permute-start | bytes 442376 | tf_op jit(solution)/shard_map/ppermute | solution.py:32
  42.5 19.6 %collective-permute-start.7 = (bf16[288,256]{1,0:T(8,128)(2,1)S(1)}, bf16[288,256]{1,0:T(8,128)(2,1)S(1)}, u32[]{:S(2)}, u32[]{:S(2)}) collective-permute-start(bf16[288,256]{1,0:T(8,128)(2,1)S(1)} %get-tuple-element.39), channel_id=1, source_target_pairs={{1,0},{2,1},{3,2},{4,3},{5,4},{6,5},{7,6},{8,7},{9,8},{10,9},{11,1... | collective-permute-start | bytes 442376 | tf_op jit(solution)/shard_map/ppermute | solution.py:32
  44.9 17.3 %collective-permute-start.8 = (bf16[288,256]{1,0:T(8,128)(2,1)S(1)}, bf16[288,256]{1,0:T(8,128)(2,1)S(1)}, u32[]{:S(2)}, u32[]{:S(2)}) collective-permute-start(bf16[288,256]{1,0:T(8,128)(2,1)S(1)} %get-tuple-element.40), channel_id=1, source_target_pairs={{2,0},{3,1},{4,2},{5,3},{6,4},{7,5},{8,6},{9,7},{10,8},{11,9},{12,... | collective-permute-start | bytes 442376 | tf_op jit(solution)/shard_map/ppermute | solution.py:32
  48.3 13.9 %collective-permute-start.9 = (bf16[288,256]{1,0:T(8,128)(2,1)S(1)}, bf16[288,256]{1,0:T(8,128)(2,1)S(1)}, u32[]{:S(2)}, u32[]{:S(2)}) collective-permute-start(bf16[288,256]{1,0:T(8,128)(2,1)S(1)} %get-tuple-element.41), channel_id=1, source_target_pairs={{3,0},{4,1},{5,2},{6,3},{7,4},{8,5},{9,6},{10,7},{11,8},{12,9},{13... | collective-permute-start | bytes 442376 | tf_op jit(solution)/shard_map/ppermute | solution.py:32
